TPU v7x, 32 devices: a whole 2x2x4 slice. The times are simulated.
32 devices in a mesh: heads: 4 (over y, x), docs: 8 (over z, core).
Axes of the slice: x: 2, y: 2, z: 4, core: 2. Of those that a mesh axis runs over, the one named last changes fastest.
Arguments:
- query_rows: bfloat16 [4096, 4096], P('docs', 'heads'), may hold values from -40 to 40
- key_rows: bfloat16 [4096, 512], P('docs', 'heads'), may hold values from -4.5 to 4.5
- value_rows: bfloat16 [4096, 512], P('docs', 'heads'), may hold values from -6 to 6
- doc_blocks: int32 [4], replicated, may hold values from 1 to 16, 32 in all
- out_weight: bfloat16 [4096, 2048], P('heads', 'docs'), may hold values from -0.125 to 0.125
Outputs:
- mixed: bfloat16 [4096, 2048], P('docs', 'heads')
All inputs are finite; a program needn't handle non-finite values.
Results may differ from a plain program's by a relative error of at most 0.0095.
Values may be sent and summed in bfloat16 or wider, within the bound.
No kernel may reach another device: no remote copies, remote signals or barrier semaphores. Data moves between devices by JAX's collectives and lax.ppermute only.
A program may use at most 64 MiB of HBM per device.

v0:
```python
import jax
import jax.numpy as jnp
from jax import lax
from jax.sharding import PartitionSpec as P

HD = 128
BLOCK = 128
MOSTB = 16


def from_behind(block, axis, distance):
    devices = range(lax.axis_size(axis))
    route = [(i - distance, i) for i in devices if i - distance in devices]
    return lax.ppermute(block, axis, route)


def local(query_rows, key_rows, value_rows, doc_blocks, out_weight):
    local_tokens = query_rows.shape[0]
    head_size = key_rows.shape[1]
    first_token = lax.axis_index("docs") * local_tokens
    reach = (MOSTB - 1) * BLOCK
    shard_count = (reach + local_tokens - 1) // local_tokens
    key_pieces = []
    value_pieces = []
    for distance in range(shard_count, 0, -1):
        needed = min(local_tokens, reach - (distance - 1) * local_tokens)
        tail_pair = jnp.stack(
            [key_rows[local_tokens - needed :], value_rows[local_tokens - needed :]]
        )
        before = from_behind(tail_pair, "docs", distance)
        key_pieces.append(before[0])
        value_pieces.append(before[1])
    ext_keys = jnp.concatenate(key_pieces + [key_rows], axis=0)
    ext_values = jnp.concatenate(value_pieces + [value_rows], axis=0)
    rim_rows = ext_keys.shape[0] - local_tokens
    doc_ends = jnp.cumsum(doc_blocks) * BLOCK
    positions = first_token - rim_rows + jnp.arange(rim_rows + local_tokens, dtype=jnp.int32)
    doc_ids = jnp.sum((doc_ends[None, :] <= positions[:, None]).astype(jnp.int32), axis=1)
    doc_ids = jnp.where(positions < 0, -1, doc_ids)
    query_block = min(512, local_tokens)
    window = reach + query_block
    offset = rim_rows - reach
    heads_here = query_rows.shape[1] // head_size
    head_pack = min(4, heads_here)
    pack_count = heads_here // head_pack
    block_count = local_tokens // query_block
    score_scale = HD ** (-0.5)

    def one_block(block_index):
        block_number = block_index // pack_count
        pack_index = block_index % pack_count
        first_row = block_number * query_block
        query_part = lax.dynamic_slice(
            query_rows,
            (first_row, pack_index * head_pack * head_size),
            (query_block, head_pack * head_size),
        ).reshape(query_block, head_pack, head_size)
        query_doc = lax.dynamic_slice_in_dim(doc_ids, first_row + rim_rows, query_block, 0)
        query_pos = first_row + rim_rows + jnp.arange(query_block, dtype=jnp.int32)
        key_pos = first_row + offset + jnp.arange(window, dtype=jnp.int32)
        allowed = (query_doc[:, None] == doc_ids[None, :]) & (
            key_pos[None, :] <= query_pos[:, None]
        )
        scores = (
            jnp.einsum("qhd,kd->hqk", query_part, ext_keys, preferred_element_type=jnp.float32)
            * score_scale
        )
        scores = jnp.where(allowed[None], scores, -jnp.inf)
        row_max = jnp.max(scores, axis=-1, keepdims=True)
        raised = jnp.exp(scores - row_max)
        row_sum = jnp.sum(raised, axis=-1)
        probs = raised.astype(jnp.bfloat16)
        mixed = jnp.einsum("hqk,kd->qhd", probs, ext_values, preferred_element_type=jnp.float32)
        mixed = mixed / jnp.transpose(row_sum)[:, :, None]
        return mixed.astype(jnp.bfloat16).reshape(query_block, head_pack * head_size)

    blocks = lax.map(one_block, jnp.arange(block_count * pack_count, dtype=jnp.int32))
    attended = blocks.reshape(block_count, pack_count, query_block, head_pack * head_size)
    attended = jnp.transpose(attended, (0, 2, 1, 3)).reshape(local_tokens, heads_here * head_size)
    partial_value = jnp.dot(
        attended,
        lax.all_gather(out_weight, "docs", axis=1, tiled=True),
        preferred_element_type=jnp.float32,
    )
    summed = lax.psum_scatter(
        partial_value.astype(jnp.bfloat16), "heads", scatter_dimension=1, tiled=True
    )
    return summed


def solution(mesh):
    placed = (P("docs", "heads"), P("docs", "heads"), P("docs", "heads"), P(), P("heads", "docs"))
    return jax.shard_map(
        local, mesh=mesh, in_specs=placed, out_specs=P("docs", "heads"), check_vma=False
    )
```

profile of v0, /device:TPU:16, one launch (start us, length us, event | category | flops | bytes accessed | tf_op | source)
XLA Modules:
  0.0 163.3 jit_solution(1700925412164845691)
XLA Ops:
  6.5 1.0 copy.23
  7.5 1.0 copy.24
  8.6 2.9 %collective-permute-start.1 = (bf16[2,512,128]{1,2,0:T(8,128)(2,1)S(1)}, bf16[2,512,128]{1,2,0:T(8,128)(2,1)S(1)}, u32[]{:S(2)}, u32[]{:S(2)}) collective-permute-start(bf16[2,512,128]{1,2,0:T(8,128)(2,1)S(1)} %pad_maximum_fusion), channel_id=1, source_target_pairs={{0,3},{1,4},{2,5},{3,6},{4,7},{8,11},{9,12},{10,13},{11,14},{12,15... | collective-permute-start | bytes 786440 | tf_op jit(solution)/shard_map/ppermute | solution.py:14
  11.5 1.9 %collective-permute-start.2 = (bf16[2,512,128]{1,2,0:T(8,128)(2,1)S(1)}, bf16[2,512,128]{1,2,0:T(8,128)(2,1)S(1)}, u32[]{:S(2)}, u32[]{:S(2)}) collective-permute-start(bf16[2,512,128]{1,2,0:T(8,128)(2,1)S(1)} %pad_maximum_fusion), channel_id=1, source_target_pairs={{0,2},{1,3},{2,4},{3,5},{4,6},{5,7},{8,10},{9,11},{10,12},{11,13},... | collective-permute-start | bytes 786440 | tf_op jit(solution)/shard_map/ppermute | solution.py:14
  13.5 1.9 %collective-permute-start.3 = (bf16[2,512,128]{1,2,0:T(8,128)(2,1)S(1)}, bf16[2,512,128]{1,2,0:T(8,128)(2,1)S(1)}, u32[]{:S(2)}, u32[]{:S(2)}) collective-permute-start(bf16[2,512,128]{1,2,0:T(8,128)(2,1)S(1)} %pad_maximum_fusion), channel_id=1, source_target_pairs={{0,1},{1,2},{2,3},{3,4},{4,5},{5,6},{6,7},{8,9},{9,10},{10,11},{11... | collective-permute-start | bytes 786440 | tf_op jit(solution)/shard_map/ppermute | solution.py:14
  15.5 1.3 collective-permute-start
  17.8 10.5 %collective-permute-done = bf16[2,384,128]{1,2,0:T(8,128)(2,1)S(1)} collective-permute-done((bf16[2,384,128]{1,2,0:T(8,128)(2,1)S(1)}, bf16[2,384,128]{1,2,0:T(8,128)(2,1)S(1)}, u32[]{:S(2)}, u32[]{:S(2)}) %collective-permute-start) | collective-permute-done | bytes 196640 | tf_op jit(solution)/shard_map/ppermute | solution.py:14
  28.4 7.9 %collective-permute-done.2 = bf16[2,512,128]{1,2,0:T(8,128)(2,1)S(1)} collective-permute-done((bf16[2,512,128]{1,2,0:T(8,128)(2,1)S(1)}, bf16[2,512,128]{1,2,0:T(8,128)(2,1)S(1)}, u32[]{:S(2)}, u32[]{:S(2)}) %collective-permute-start.2) | collective-permute-done | bytes 262176 | tf_op jit(solution)/shard_map/ppermute | solution.py:14
  36.2 25.7 %collective-permute-done.3 = bf16[2,512,128]{1,2,0:T(8,128)(2,1)S(1)} collective-permute-done((bf16[2,512,128]{1,2,0:T(8,128)(2,1)S(1)}, bf16[2,512,128]{1,2,0:T(8,128)(2,1)S(1)}, u32[]{:S(2)}, u32[]{:S(2)}) %collective-permute-start.3) | collective-permute-done | bytes 262176 | tf_op jit(solution)/shard_map/ppermute | solution.py:14
  62.4 45.2 %while.12 = (s32[]{:T(128)}, bf16[2,512,512]{1,2,0:T(8,128)(2,1)}, s32[2]{0:T(128)S(1)}, s32[2432]{0:T(1024)S(1)}, bf16[512,1024]{1,0:T(8,128)(2,1)}, /*index=5*...) while((s32[]{:T(128)}, bf16[2,512,512]{1,2,0:T(8,128)(2,1)}, ...), condition=%wide.region_5.6_spmd, body=%wide.region_2.5_spmd.sunk | while | flops 2609183744 | bytes 78658568 | solution.py:77
  65.9 1.1 compare_and_fusion.2
  67.0 1.1 constant_dynamic-slice_fusion.2
  68.3 5.0 %bitcast_reduce_fusion.2 = (f32[4,512]{1,0:T(4,128)S(1)}, f32[512,4,2432]{2,0,1:T(8,128)S(1)}) fusion(pred[512,2432]{1,0:T(8,128)(4,1)S(1)} %compare_and_fusion.2, bf16[512,4,128]{0,2,1:T(8,128)(2,1)S(1)} %bitcast.101, bf16[2432,128]{1,0:T(8,128)(2,1)S(1)} %get-tuple-element.229), kind=kOutput, calls=%fused_computation.1.clone.1 | convolution fusion | flops 1290008576 | bytes 22323200 | tf_op jit(solution)/shard_map/while/body/eval_jaxpr/qhd,kd->hqk/dot_general | solution.py:65
  73.3 5.2 %fusion.34 = f32[4,512]{1,0:T(4,128)S(1)} fusion(f32[512,4,2432]{2,0,1:T(8,128)S(1)} %get-tuple-element.192, f32[4,512]{1,0:T(4,128)S(1)} %get-tuple-element.193, pred[512,2432]{1,0:T(8,128)(4,1)S(1)} %compare_and_fusion.2), kind=kLoop, calls=%fused_computation.4.clone.1 | loop fusion | flops 19920896 | bytes 21184512 | tf_op jit(solution)/shard_map/while/body/eval_jaxpr/reduce_sum | solution.py:71
  78.4 5.5 %divide_convert_fusion.2 = bf16[512,4,128]{0,2,1:T(8,128)(2,1)S(1)} fusion(f32[512,4,2432]{2,0,1:T(8,128)S(1)} %get-tuple-element.192, f32[4,512]{1,0:T(4,128)S(1)} %get-tuple-element.193, pred[512,2432]{1,0:T(8,128)(4,1)S(1)} %compare_and_fusion.2, bf16[2432,128]{0,1:T(8,128)(2,1)S(1)} %get-tuple-element.230, f32[512,4]{0,1:T(4,128)S(1)} %bitcast.105), kind=kOutput, calls=%fused_computation.10.clone.1 | convolution fusion | flops 1295515648 | bytes 22331392 | tf_op jit(solution)/shard_map/while/body/eval_jaxpr/hqk,kd->qhd/dot_general | solution.py:73
  84.0 1.0 copy-done.1
  88.5 1.1 compare_and_fusion.2
  89.6 1.1 constant_dynamic-slice_fusion.2
  90.9 5.0 %bitcast_reduce_fusion.2 = (f32[4,512]{1,0:T(4,128)S(1)}, f32[512,4,2432]{2,0,1:T(8,128)S(1)}) fusion(pred[512,2432]{1,0:T(8,128)(4,1)S(1)} %compare_and_fusion.2, bf16[512,4,128]{0,2,1:T(8,128)(2,1)S(1)} %bitcast.101, bf16[2432,128]{1,0:T(8,128)(2,1)S(1)} %get-tuple-element.229), kind=kOutput, calls=%fused_computation.1.clone.1 | convolution fusion | flops 1290008576 | bytes 22323200 | tf_op jit(solution)/shard_map/while/body/eval_jaxpr/qhd,kd->hqk/dot_general | solution.py:65
  95.9 5.2 %fusion.34 = f32[4,512]{1,0:T(4,128)S(1)} fusion(f32[512,4,2432]{2,0,1:T(8,128)S(1)} %get-tuple-element.192, f32[4,512]{1,0:T(4,128)S(1)} %get-tuple-element.193, pred[512,2432]{1,0:T(8,128)(4,1)S(1)} %compare_and_fusion.2), kind=kLoop, calls=%fused_computation.4.clone.1 | loop fusion | flops 19920896 | bytes 21184512 | tf_op jit(solution)/shard_map/while/body/eval_jaxpr/reduce_sum | solution.py:71
  101.0 5.5 %divide_convert_fusion.2 = bf16[512,4,128]{0,2,1:T(8,128)(2,1)S(1)} fusion(f32[512,4,2432]{2,0,1:T(8,128)S(1)} %get-tuple-element.192, f32[4,512]{1,0:T(4,128)S(1)} %get-tuple-element.193, pred[512,2432]{1,0:T(8,128)(4,1)S(1)} %compare_and_fusion.2, bf16[2432,128]{0,1:T(8,128)(2,1)S(1)} %get-tuple-element.230, f32[512,4]{0,1:T(4,128)S(1)} %bitcast.105), kind=kOutput, calls=%fused_computation.10.clone.1 | convolution fusion | flops 1295515648 | bytes 22331392 | tf_op jit(solution)/shard_map/while/body/eval_jaxpr/hqk,kd->qhd/dot_general | solution.py:73
  106.6 1.0 copy-done.1
  107.6 6.2 %convolution_convert_fusion = bf16[512,2048]{1,0:T(8,128)(2,1)} fusion(bf16[512,1024]{0,1:T(8,128)(2,1)} %bitcast.106, bf16[1024,2048]{1,0:T(8,128)(2,1)} %all-gather.2.cloned.1.call-done), kind=kOutput, calls=%fused_computation.20 | convolution fusion | flops 2148532224 | bytes 7340032 | tf_op jit(solution)/shard_map/dot_general | solution.py:80
  113.9 42.6 %reduce-scatter.2.cloned.1.call-done = bf16[512,512]{1,0:T(8,128)(2,1)} async-done(((bf16[512,2048]{1,0:T(8,128)(2,1)}), bf16[512,512]{1,0:T(8,128)(2,1)}) %reduce-scatter.2.cloned.1.call-update) | async-done | bytes 524304 | tf_op jit(solution)/shard_map/reduce_scatter | solution.py:85
  (41 shorter events, 3.5 us)
Async XLA Ops:
  6.5 101.1 %all-gather.2.cloned.1.call-start = ((), (), s32[]{:S(2)}) async-start(), calls=%async_computation.1 | async-start | bytes 4718592 | tf_op jit(solution)/shard_map/all_gather | solution.py:82
  8.6 19.7 %collective-permute-start.1 = (bf16[2,512,128]{1,2,0:T(8,128)(2,1)S(1)}, bf16[2,512,128]{1,2,0:T(8,128)(2,1)S(1)}, u32[]{:S(2)}, u32[]{:S(2)}) collective-permute-start(bf16[2,512,128]{1,2,0:T(8,128)(2,1)S(1)} %pad_maximum_fusion), channel_id=1, source_target_pairs={{0,3},{1,4},{2,5},{3,6},{4,7},{8,11},{9,12},{10,13},{11,14},{12,15... | collective-permute-start | bytes 786440 | tf_op jit(solution)/shard_map/ppermute | solution.py:14
  11.5 24.7 %collective-permute-start.2 = (bf16[2,512,128]{1,2,0:T(8,128)(2,1)S(1)}, bf16[2,512,128]{1,2,0:T(8,128)(2,1)S(1)}, u32[]{:S(2)}, u32[]{:S(2)}) collective-permute-start(bf16[2,512,128]{1,2,0:T(8,128)(2,1)S(1)} %pad_maximum_fusion), channel_id=1, source_target_pairs={{0,2},{1,3},{2,4},{3,5},{4,6},{5,7},{8,10},{9,11},{10,12},{11,13},... | collective-permute-start | bytes 786440 | tf_op jit(solution)/shard_map/ppermute | solution.py:14
  13.5 48.5 %collective-permute-start.3 = (bf16[2,512,128]{1,2,0:T(8,128)(2,1)S(1)}, bf16[2,512,128]{1,2,0:T(8,128)(2,1)S(1)}, u32[]{:S(2)}, u32[]{:S(2)}) collective-permute-start(bf16[2,512,128]{1,2,0:T(8,128)(2,1)S(1)} %pad_maximum_fusion), channel_id=1, source_target_pairs={{0,1},{1,2},{2,3},{3,4},{4,5},{5,6},{6,7},{8,9},{9,10},{10,11},{11... | collective-permute-start | bytes 786440 | tf_op jit(solution)/shard_map/ppermute | solution.py:14
  15.5 12.8 %collective-permute-start = (bf16[2,384,128]{1,2,0:T(8,128)(2,1)S(1)}, bf16[2,384,128]{1,2,0:T(8,128)(2,1)S(1)}, u32[]{:S(2)}, u32[]{:S(2)}) collective-permute-start(bf16[2,384,128]{1,2,0:T(8,128)(2,1)S(1)} %pad_maximum_fusion.1), channel_id=1, source_target_pairs={{0,4},{1,5},{2,6},{3,7},{8,12},{9,13},{10,14},{11,15},{16,20},{17,... | collective-permute-start | bytes 589832 | tf_op jit(solution)/shard_map/ppermute | solution.py:14
  16.8 139.6 %reduce-scatter.2.cloned.1.call-start = ((), (), s32[]{:S(2)}) async-start(), calls=%async_computation.2 | async-start | bytes 2621440 | tf_op jit(solution)/shard_map/reduce_scatter | solution.py:85
  78.4 5.5 %copy-start = (bf16[2,512,512]{1,2,0:T(8,128)(2,1)S(1)}, bf16[2,512,512]{1,2,0:T(8,128)(2,1)}, u32[]{:S(2)}) copy-start(bf16[2,512,512]{1,2,0:T(8,128)(2,1)} %get-tuple-element.210) | copy-start | bytes 3145732 | tf_op jit(solution)/shard_map/while
  84.0 1.0 copy-start.1
  101.0 5.5 %copy-start = (bf16[2,512,512]{1,2,0:T(8,128)(2,1)S(1)}, bf16[2,512,512]{1,2,0:T(8,128)(2,1)}, u32[]{:S(2)}) copy-start(bf16[2,512,512]{1,2,0:T(8,128)(2,1)} %get-tuple-element.210) | copy-start | bytes 3145732 | tf_op jit(solution)/shard_map/while
  106.6 1.0 copy-start.1
Sparse Core Ops, SparseCore 0:
  16.9 59.3 all-gather.1
  114.0 42.3 reduce-scatter.1
where the time goes:
time: 165 us; the launch traced here: 163 us
  waiting for transfers between devices  86.7 us (53%)
  matrix products  27.2 us (16%)
  between operations  13.6 us (8%)
  other arithmetic  13.4 us (8%)
  local copies, waits for them, and re-layouts  8.57 us (5%)
  starting transfers between devices  8.1 us (5%)
  loops' own time  5.67 us (3%)
    ppermute x4, waiting for transfers between devices, from_behind(): return lax.ppermute(block, axis, route)  44.1 us
    reduce_scatter x1, waiting for transfers between devices, local(): lax.psum_scatter(partial_value.astype(jnp.bfloat16), 'heads', scatter_dim...  42.6 us
    dot_general x2, matrix products, one_block(): jnp.einsum('hqk,kd->qhd', probs, ext_values, preferred_element_type=jnp.f...  11 us
    reduce_sum x2, other arithmetic, one_block(): row_sum = jnp.sum(raised, axis=-1)  10.3 us
    dot_general x2, matrix products, one_block(): jnp.einsum('qhd,kd->hqk', query_part, ext_keys, preferred_element_type=jn...  9.98 us
    ppermute x4, starting transfers between devices, from_behind(): return lax.ppermute(block, axis, route)  8.06 us
    dot_general x1, matrix products, local(): jnp.dot(attended, lax.all_gather(out_weight, 'docs', axis=1, tiled=True),...  6.21 us
    another operation x1, loops' own time, local(): lax.map(one_block, jnp.arange(block_count * pack_count, dtype=jnp.int32))  5.67 us
  transfers between devices with their start and end apart: 6, of which 4 were waited for; matrix products, arithmetic and copies ran while one was open for 24% of the time, Pallas kernels for 0%

commit v1 on v0

v1 whole, which is shorter than its diff:
```python
import functools
import jax
import jax.numpy as jnp
from jax import lax
from jax.experimental import pallas as pl
from jax.experimental.pallas import tpu as pltpu
from jax.sharding import PartitionSpec as P

HD = 128
BLOCK = 128
MOSTB = 16
STEP = 4
MASKED = -1e30
EXP2_SCALE = HD ** (-0.5) * 1.4426950408889634


def attend(meta, docs, query, own, other, near, far, out, keys, values, stacked, scores, peak, total):
    tokens = query.shape[0]
    heads = query.shape[1] // HD
    rows = heads * BLOCK
    span = STEP * BLOCK
    shard = meta[0]
    odd = lax.rem(shard, 2)
    blocks = tokens // BLOCK

    def place(index, piece):
        start = pl.multiple_of(index * tokens, BLOCK)
        keys[pl.ds(start, tokens), :] = piece[0]
        values[pl.ds(start, tokens), :HD] = piece[1]

    values[:, HD:] = jnp.ones((values.shape[0], HD), values.dtype)
    place(0, far.at[1])
    place(1, far.at[0])
    place(2, near.at[0])
    place(3, near.at[1])
    place(4 + odd, own)
    place(5 - odd, other)

    def one_block(row, carry):
        place_in = shard * blocks + row
        begin = jnp.int32(0)
        edge = jnp.int32(0)
        for doc in range(docs.shape[0]):
            edge = edge + docs[doc]
            begin = jnp.where(edge <= place_in, edge, begin)
        count = place_in - begin + 1
        steps = lax.div(count + STEP - 1, STEP)
        last = (4 + odd) * blocks + row
        first_row = pl.multiple_of(row * BLOCK, BLOCK)
        for head in range(heads):
            stacked[head * BLOCK : (head + 1) * BLOCK, :] = query[
                pl.ds(first_row, BLOCK), head * HD : (head + 1) * HD
            ]

        def score(step, masked):
            start = pl.multiple_of((last - step * STEP - (STEP - 1)) * BLOCK, BLOCK)
            part = keys[pl.ds(start, span), :]
            column = pl.multiple_of(step * span, span)
            for head in range(heads):
                here = slice(head * BLOCK, (head + 1) * BLOCK)
                got = lax.dot_general(
                    stacked[here, :], part, (((1,), (1,)), ((), ())),
                    preferred_element_type=jnp.float32,
                )
                high = None
                for block in range(STEP):
                    piece = got[:, block * BLOCK : (block + 1) * BLOCK]
                    if masked:
                        back = step * STEP + (STEP - 1 - block)
                        keep = jnp.broadcast_to(back < count, piece.shape)
                        if block == STEP - 1:
                            down = lax.broadcasted_iota(jnp.int32, piece.shape, 0)
                            across = lax.broadcasted_iota(jnp.int32, piece.shape, 1)
                            keep = keep & ((across <= down) | (step > 0))
                        piece = jnp.where(keep, piece, MASKED)
                    scores[here, pl.ds(pl.multiple_of(column + block * BLOCK, BLOCK), BLOCK)] = piece
                    high = piece if high is None else jnp.maximum(high, piece)
                peak[here, :] = jnp.maximum(peak[here, :], high)

        peak[...] = jnp.full(peak.shape, MASKED, jnp.float32)
        score(jnp.int32(0), True)

        def middle(step, carry):
            score(step, False)
            return carry

        lax.fori_loop(1, steps - 1, middle, 0)

        @pl.when(steps > 1)
        def _():
            score(steps - 1, True)

        for head in range(heads):
            here = slice(head * BLOCK, (head + 1) * BLOCK)
            peak[here, :] = jnp.broadcast_to(
                jnp.max(peak[here, :], axis=1, keepdims=True), (BLOCK, BLOCK)
            )
        total[...] = jnp.zeros(total.shape, jnp.float32)

        def weigh(step, carry):
            start = pl.multiple_of((last - step * STEP - (STEP - 1)) * BLOCK, BLOCK)
            part = values[pl.ds(start, span), :]
            column = pl.multiple_of(step * span, span)
            for head in range(heads):
                here = slice(head * BLOCK, (head + 1) * BLOCK)
                top = jnp.concatenate([peak[here, :]] * STEP, axis=1)
                raised = jnp.exp2((scores[here, pl.ds(column, span)] - top) * EXP2_SCALE)
                total[here, :] += jnp.dot(
                    raised.astype(jnp.bfloat16), part, preferred_element_type=jnp.float32
                )
            return carry

        lax.fori_loop(0, steps, weigh, 0)
        for head in range(heads):
            here = slice(head * BLOCK, (head + 1) * BLOCK)
            out[pl.ds(first_row, BLOCK), head * HD : (head + 1) * HD] = (
                total[here, :HD] / total[here, HD:]
            ).astype(out.dtype)
        return carry

    lax.fori_loop(0, blocks, one_block, 0)


def attention(shard, docs, query, own, other, near, far):
    tokens, width = query.shape
    rows = width // HD * BLOCK
    vmem = pl.BlockSpec(memory_space=pltpu.VMEM)
    smem = pl.BlockSpec(memory_space=pltpu.SMEM)
    return pl.pallas_call(
        attend,
        out_shape=jax.ShapeDtypeStruct((tokens, width), jnp.bfloat16),
        in_specs=[smem, smem] + [vmem] * 5,
        out_specs=vmem,
        scratch_shapes=[
            pltpu.VMEM((6 * tokens, HD), jnp.bfloat16),
            pltpu.VMEM((6 * tokens, 2 * HD), jnp.bfloat16),
            pltpu.VMEM((rows, HD), jnp.bfloat16),
            pltpu.VMEM((rows, MOSTB * BLOCK), jnp.float32),
            pltpu.VMEM((rows, BLOCK), jnp.float32),
            pltpu.VMEM((rows, 2 * HD), jnp.float32),
        ],
        name="attend",
    )(shard, docs, query, own, other, near, far)


def project(attended, weight, order):
    tokens, depth = attended.shape
    count = order.shape[0]
    width = weight.shape[1] // 4

    def body(order_ref, left, right, out):
        out[0] = jnp.dot(left[...], right[...], preferred_element_type=jnp.float32).astype(out.dtype)

    return pl.pallas_call(
        body,
        out_shape=jax.ShapeDtypeStruct((count, tokens, width), jnp.bfloat16),
        grid_spec=pltpu.PrefetchScalarGridSpec(
            num_scalar_prefetch=1,
            grid=(count,),
            in_specs=[
                pl.BlockSpec((tokens, depth), lambda i, order: (0, 0)),
                pl.BlockSpec((depth, width), lambda i, order: (0, order[i])),
            ],
            out_specs=pl.BlockSpec((1, tokens, width), lambda i, order: (i, 0, 0)),
        ),
        name="project",
    )(order, attended, weight)


def build(shards, groups):
    def swap_core(block):
        return lax.ppermute(block, "docs", [(i, i ^ 1) for i in range(shards)])

    def exchange(block, first):
        route = []
        for group in range(groups):
            for shard in range(shards):
                flip = 1 if (shard % 2 == 0) == first else 2
                route.append((group * shards + shard, (group ^ flip) * shards + shard))
        return lax.ppermute(block, ("heads", "docs"), route)

    def local(query_rows, key_rows, value_rows, doc_blocks, out_weight):
        shard = lax.axis_index("docs")
        group = lax.axis_index("heads")
        own = jnp.stack([key_rows, value_rows])
        other = swap_core(own)
        pair = jnp.stack([own, other])
        route = []
        for i in range(shards):
            target = i + (4 if i % 2 else 2)
            if target < shards:
                route.append((i, target))
        came = lax.ppermute(pair, "docs", route)
        crossed = swap_core(came)
        odd = shard % 2 == 1
        near = jnp.where(odd, crossed, came)
        far = jnp.where(odd, came, crossed)
        attended = attention(
            jnp.reshape(shard, (1,)).astype(jnp.int32), doc_blocks, query_rows, own, other, near, far
        )
        weight = lax.all_gather(out_weight, "docs", axis=1, tiled=True)
        first = jnp.where(odd, 2, 1)
        second = 3 - first
        send = project(attended, weight, jnp.stack([group ^ first, group ^ 3]).astype(jnp.int32))
        arrived = exchange(send, True)
        keep = project(attended, weight, jnp.stack([group, group ^ second]).astype(jnp.int32))
        f32 = jnp.float32
        onward = (keep[1].astype(f32) + arrived[1].astype(f32)).astype(jnp.bfloat16)
        final = exchange(onward, False)
        return (keep[0].astype(f32) + arrived[0].astype(f32) + final.astype(f32)).astype(jnp.bfloat16)

    return local


def solution(mesh):
    placed = (P("docs", "heads"), P("docs", "heads"), P("docs", "heads"), P(), P("heads", "docs"))
    local = build(mesh.shape["docs"], mesh.shape["heads"])
    return jax.shard_map(
        local, mesh=mesh, in_specs=placed, out_specs=P("docs", "heads"), check_vma=False
    )
```

time: 165 us -> 118 us (0.72); the launches traced: 163 us -> 119 us
  matrix products: 27.2 us -> 0 us
  Pallas kernels: 0 us -> 27 us
  waiting for transfers between devices: 86.7 us -> 65.3 us
  local copies, waits for them, and re-layouts: 8.57 us -> 0.01 us
  other arithmetic: 13.4 us -> 6.55 us
  loops' own time: 5.67 us -> 0 us
    reduce_scatter x1 -> x0, waiting for transfers between devices: 42.6 us -> none  [local(): lax.psum_scatter(partial_value.astype(jnp.bfloat16), 'heads', scatter_dim...]
    dot_general x5 -> x0, matrix products: 27.2 us -> none  [the longest x2 11 us: one_block(): jnp.einsum('hqk,kd->qhd', probs, ext_values, preferred_element_type=jnp.f...]
    pallas_call x0 -> x3, Pallas kernels: none -> 27 us  [the longest x1 18 us: attention(): pl.pallas_call(attend, out_shape=jax.ShapeDtypeStruct((tokens, width), jn...]
    ppermute x4 -> x5, waiting for transfers between devices: 44.1 us -> 64.6 us  [the longest x1 44.6 us: local(): came = lax.ppermute(pair, 'docs', route)]
    reduce_sum x3 -> x0, other arithmetic: 10.4 us -> none  [the longest x2 10.3 us: one_block(): row_sum = jnp.sum(raised, axis=-1)]
    another operation x1 -> x0, loops' own time: 5.67 us -> none  [local(): lax.map(one_block, jnp.arange(block_count * pack_count, dtype=jnp.int32))]
    dynamic_slice x8 -> x0, local copies, waits for them, and re-layouts: 4.05 us -> none  [the longest x4 2.59 us: one_block(): lax.dynamic_slice(query_rows, (first_row, pack_index * head_pack * head_s...]
    convert_element_type x0 -> x2, other arithmetic: none -> 3.21 us  [the longest x1 2.04 us: local(): (keep[0].astype(f32) + arrived[0].astype(f32) + final.astype(f32)).astype...]
  transfers between devices with their start and end apart: 6 -> 6, of which waited for: 4 -> 5; matrix products, arithmetic and copies ran while one was open for 24% -> 3% of each run, Pallas kernels for 0% -> 19%
where the time goes in v1:
time: 118 us; the launch traced here: 119 us
  waiting for transfers between devices  65.3 us (55%)
  Pallas kernels  27 us (23%)
  between operations  13.4 us (11%)
  other arithmetic  6.55 us (6%)
  starting transfers between devices  6.53 us (6%)
    ppermute x1, waiting for transfers between devices, local(): came = lax.ppermute(pair, 'docs', route)  44.6 us
    pallas_call x1, Pallas kernels, attention(): pl.pallas_call(attend, out_shape=jax.ShapeDtypeStruct((tokens, width), jn...  18 us
    ppermute x2, waiting for transfers between devices, exchange(): return lax.ppermute(block, ('heads', 'docs'), route)  17.3 us
    pallas_call x2, Pallas kernels, project(): pl.pallas_call(body, out_shape=jax.ShapeDtypeStruct((count, tokens, width...  8.94 us
    ppermute x1, starting transfers between devices, local(): came = lax.ppermute(pair, 'docs', route)  3.48 us
    ppermute x2, starting transfers between devices, exchange(): return lax.ppermute(block, ('heads', 'docs'), route)  2.97 us
    ppermute x2, waiting for transfers between devices, swap_core(): return lax.ppermute(block, 'docs', [(i, i ^ 1) for i in range(shards)])  2.77 us
  transfers between devices with their start and end apart: 6, of which 5 were waited for; matrix products, arithmetic and copies ran while one was open for 3% of the time, Pallas kernels for 19%

profile of v1, /device:TPU:16, one launch (start us, length us, event | category | flops | bytes accessed | tf_op | source)
XLA Modules:
  0.0 118.8 jit_solution(10943716077696974329)
XLA Ops:
  6.5 0.0 all-gather.2.cloned.1.call-start
  6.5 0.7 all-gather.2.cloned.1.call-update
  7.3 1.0 fusion.2
  8.3 0.0 copy-start
  8.3 0.1 collective-permute-start
  8.4 1.5 %collective-permute-done.other = bf16[2,512,128]{2,1,0:T(8,128)(2,1)S(1)} collective-permute-done((bf16[2,512,128]{2,1,0:T(8,128)(2,1)S(1)}, bf16[2,512,128]{2,1,0:T(8,128)(2,1)S(1)}, u32[]{:S(2)}, u32[]{:S(2)}) %collective-permute-start) | collective-permute-done | bytes 262176 | tf_op jit(solution)/shard_map/ppermute | solution.py:172
  9.9 0.1 pad_maximum_fusion
  9.9 3.5 %collective-permute-start.1 = (bf16[2,2,512,128]{3,2,1,0:T(8,128)(2,1)S(1)}, bf16[2,2,512,128]{3,2,1,0:T(8,128)(2,1)S(1)}, u32[]{:S(2)}, u32[]{:S(2)}) collective-permute-start(bf16[2,2,512,128]{3,2,1,0:T(8,128)(2,1)S(1)} %pad_maximum_fusion), channel_id=1, source_target_pairs={{0,2},{1,5},{2,4},{3,7},{4,6},{8,10},{9,13},{10,12},{11,15},{12,14... | collective-permute-start | bytes 1572872 | tf_op jit(solution)/shard_map/ppermute | solution.py:193
  13.4 44.6 %collective-permute-done.1 = bf16[2,2,512,128]{3,2,1,0:T(8,128)(2,1)S(1)} collective-permute-done((bf16[2,2,512,128]{3,2,1,0:T(8,128)(2,1)S(1)}, bf16[2,2,512,128]{3,2,1,0:T(8,128)(2,1)S(1)}, u32[]{:S(2)}, u32[]{:S(2)}) %collective-permute-start.1) | collective-permute-done | bytes 524320 | tf_op jit(solution)/shard_map/ppermute | solution.py:193
  58.0 0.0 collective-permute-start.2
  58.0 0.7 pad_add_fusion.1.order_ref
  58.7 1.2 %collective-permute-done.2 = bf16[2,2,512,128]{3,2,1,0:T(8,128)(2,1)S(1)} collective-permute-done((bf16[2,2,512,128]{3,2,1,0:T(8,128)(2,1)S(1)}, bf16[2,2,512,128]{3,2,1,0:T(8,128)(2,1)S(1)}, u32[]{:S(2)}, u32[]{:S(2)}) %collective-permute-start.2) | collective-permute-done | bytes 524320 | tf_op jit(solution)/shard_map/ppermute | solution.py:172
  59.9 1.1 broadcast_select_fusion
  61.0 0.0 copy-done.1
  61.0 18.0 %attend.1.left = bf16[512,1024]{1,0:T(8,128)(2,1)} custom-call(s32[1]{0:T(128)} %bitcast.2.meta, s32[4]{0:T(128)} %docs.1, bf16[512,1024]{1,0:T(8,128)(2,1)} %query.1, bf16[2,512,128]{2,1,0:T(8,128)(2,1)} %copy-done, bf16[2,512,128]{2,1,0:T(8,128)(2,1)} %copy-done.1, bf16[2,2,512,128]{3,2,1,0:T(8,128)(2,1)} %get-tuple-element.6.near, ...), custom_call_target="tpu_custom_call" | custom-call | tf_op jit(solution)/shard_map/attend/pallas_call | solution.py:129
  79.0 4.5 %project.3 = bf16[2,512,512]{2,1,0:T(8,128)(2,1)} custom-call(s32[2]{0:T(128)} %pad_add_fusion.1.order_ref, bf16[512,1024]{1,0:T(8,128)(2,1)} %attend.1.left, bf16[1024,2048]{1,0:T(8,128)(2,1)} %all-gather.2.cloned.1.call-done.right), custom_call_target="tpu_custom_call" | custom-call | tf_op jit(solution)/shard_map/project/pallas_call | solution.py:154
  83.5 1.4 %collective-permute-start.3 = (bf16[2,512,512]{2,1,0:T(8,128)(2,1)}, bf16[2,512,512]{2,1,0:T(8,128)(2,1)S(1)}, u32[]{:S(2)}, u32[]{:S(2)}) collective-permute-start(bf16[2,512,512]{2,1,0:T(8,128)(2,1)} %project.3), channel_id=1, source_target_pairs={{0,8},{1,17},{2,10},{3,19},{4,12},{5,21},{6,14},{7,23},{8,0},{9,25... | collective-permute-start | bytes 3145736 | tf_op jit(solution)/shard_map/ppermute | solution.py:180
  84.9 0.6 pad_add_fusion.order_ref
  85.5 4.5 %project.2 = bf16[2,512,512]{2,1,0:T(8,128)(2,1)} custom-call(s32[2]{0:T(128)} %pad_add_fusion.order_ref, bf16[512,1024]{1,0:T(8,128)(2,1)} %attend.1.left, bf16[1024,2048]{1,0:T(8,128)(2,1)} %all-gather.2.cloned.1.call-done.right), custom_call_target="tpu_custom_call" | custom-call | tf_op jit(solution)/shard_map/project/pallas_call | solution.py:154
  89.9 9.6 %collective-permute-done.3 = bf16[2,512,512]{2,1,0:T(8,128)(2,1)S(1)} collective-permute-done((bf16[2,512,512]{2,1,0:T(8,128)(2,1)}, bf16[2,512,512]{2,1,0:T(8,128)(2,1)S(1)}, u32[]{:S(2)}, u32[]{:S(2)}) %collective-permute-start.3) | collective-permute-done | bytes 1048608 | tf_op jit(solution)/shard_map/ppermute | solution.py:180
  99.5 1.2 fusion.1
  100.7 1.5 %collective-permute-start.4 = (bf16[512,512]{1,0:T(8,128)(2,1)S(1)}, bf16[512,512]{1,0:T(8,128)(2,1)S(1)}, u32[]{:S(2)}, u32[]{:S(2)}) collective-permute-start(bf16[512,512]{1,0:T(8,128)(2,1)S(1)} %fusion.1), channel_id=1, source_target_pairs={{0,16},{1,9},{2,18},{3,11},{4,20},{5,13},{6,22},{7,15},{8,24},{9,1... | collective-permute-start | bytes 1572872 | tf_op jit(solution)/shard_map/ppermute | solution.py:180
  102.2 7.7 %collective-permute-done.4 = bf16[512,512]{1,0:T(8,128)(2,1)S(1)} collective-permute-done((bf16[512,512]{1,0:T(8,128)(2,1)S(1)}, bf16[512,512]{1,0:T(8,128)(2,1)S(1)}, u32[]{:S(2)}, u32[]{:S(2)}) %collective-permute-start.4) | collective-permute-done | bytes 524320 | tf_op jit(solution)/shard_map/ppermute | solution.py:180
  109.9 2.0 %fusion = bf16[512,512]{1,0:T(8,128)(2,1)} fusion(bf16[512,512]{1,0:T(8,128)(2,1)S(1)} %collective-permute-done.4, bf16[2,512,512]{2,1,0:T(8,128)(2,1)S(1)} %collective-permute-done.3, bf16[2,512,512]{2,1,0:T(8,128)(2,1)} %project.2), kind=kLoop, calls=%fused_computation.1 | loop fusion | flops 1572864 | bytes 2097152 | tf_op jit(solution)/shard_map/convert_element_type | solution.py:210
  (3 shorter events, 0.0 us)
Async XLA Ops:
  6.5 72.5 %all-gather.2.cloned.1.call-start = ((), (), s32[]{:S(2)}) async-start(), calls=%async_computation | async-start | bytes 4718592 | tf_op jit(solution)/shard_map/all_gather | solution.py:201
  8.3 52.7 %copy-start = (bf16[2,512,128]{2,1,0:T(8,128)(2,1)}, bf16[2,512,128]{2,1,0:T(8,128)(2,1)S(1)}, u32[]{:S(2)}) copy-start(bf16[2,512,128]{2,1,0:T(8,128)(2,1)S(1)} %get-tuple-element.8.own) | copy-start | bytes 786436
  8.3 1.6 %collective-permute-start = (bf16[2,512,128]{2,1,0:T(8,128)(2,1)S(1)}, bf16[2,512,128]{2,1,0:T(8,128)(2,1)S(1)}, u32[]{:S(2)}, u32[]{:S(2)}) collective-permute-start(bf16[2,512,128]{2,1,0:T(8,128)(2,1)S(1)} %get-tuple-element.8.own), channel_id=1, source_target_pairs={{0,1},{1,0},{2,3},{3,2},{4,5},{5,4},{6,7},{7,6},{8,9},{9,8},{10,11... | collective-permute-start | bytes 786440 | tf_op jit(solution)/shard_map/ppermute | solution.py:172
  9.9 51.1 %copy-start.1 = (bf16[2,512,128]{2,1,0:T(8,128)(2,1)}, bf16[2,512,128]{2,1,0:T(8,128)(2,1)S(1)}, u32[]{:S(2)}) copy-start(bf16[2,512,128]{2,1,0:T(8,128)(2,1)S(1)} %collective-permute-done.other) | copy-start | bytes 786436
  9.9 48.1 %collective-permute-start.1 = (bf16[2,2,512,128]{3,2,1,0:T(8,128)(2,1)S(1)}, bf16[2,2,512,128]{3,2,1,0:T(8,128)(2,1)S(1)}, u32[]{:S(2)}, u32[]{:S(2)}) collective-permute-start(bf16[2,2,512,128]{3,2,1,0:T(8,128)(2,1)S(1)} %pad_maximum_fusion), channel_id=1, source_target_pairs={{0,2},{1,5},{2,4},{3,7},{4,6},{8,10},{9,13},{10,12},{11,15},{12,14... | collective-permute-start | bytes 1572872 | tf_op jit(solution)/shard_map/ppermute | solution.py:193
  58.0 1.9 %collective-permute-start.2 = (bf16[2,2,512,128]{3,2,1,0:T(8,128)(2,1)S(1)}, bf16[2,2,512,128]{3,2,1,0:T(8,128)(2,1)S(1)}, u32[]{:S(2)}, u32[]{:S(2)}) collective-permute-start(bf16[2,2,512,128]{3,2,1,0:T(8,128)(2,1)S(1)} %collective-permute-done.1), channel_id=1, source_target_pairs={{0,1},{1,0},{2,3},{3,2},{4,5},{5,4},{6,7},{7,6},{8,9},{9,8},{10,11... | collective-permute-start | bytes 1572872 | tf_op jit(solution)/shard_map/ppermute | solution.py:172
  83.5 16.0 %collective-permute-start.3 = (bf16[2,512,512]{2,1,0:T(8,128)(2,1)}, bf16[2,512,512]{2,1,0:T(8,128)(2,1)S(1)}, u32[]{:S(2)}, u32[]{:S(2)}) collective-permute-start(bf16[2,512,512]{2,1,0:T(8,128)(2,1)} %project.3), channel_id=1, source_target_pairs={{0,8},{1,17},{2,10},{3,19},{4,12},{5,21},{6,14},{7,23},{8,0},{9,25... | collective-permute-start | bytes 3145736 | tf_op jit(solution)/shard_map/ppermute | solution.py:180
  100.7 9.2 %collective-permute-start.4 = (bf16[512,512]{1,0:T(8,128)(2,1)S(1)}, bf16[512,512]{1,0:T(8,128)(2,1)S(1)}, u32[]{:S(2)}, u32[]{:S(2)}) collective-permute-start(bf16[512,512]{1,0:T(8,128)(2,1)S(1)} %fusion.1), channel_id=1, source_target_pairs={{0,16},{1,9},{2,18},{3,11},{4,20},{5,13},{6,22},{7,15},{8,24},{9,1... | collective-permute-start | bytes 1572872 | tf_op jit(solution)/shard_map/ppermute | solution.py:180
Sparse Core Ops, SparseCore 0:
  8.9 61.4 all-gather.1

commit v2 on v1

v2 whole, which is shorter than its diff:
```python
import functools
import jax
import jax.numpy as jnp
from jax import lax
from jax.experimental import pallas as pl
from jax.experimental.pallas import tpu as pltpu
from jax.sharding import PartitionSpec as P

HD = 128
BLOCK = 128
MOSTB = 16
STEP = 4
MASKED = -1e30
EXP2_SCALE = HD ** (-0.5) * 1.4426950408889634
VMEM = pl.BlockSpec(memory_space=pltpu.VMEM)
SMEM = pl.BlockSpec(memory_space=pltpu.SMEM)
ANY = pl.BlockSpec(memory_space=pl.ANY)


def gather_rows(own, other, near, near_other, far, far_other, keys, values):
    tokens = own.shape[1]
    odd = lax.rem(lax.axis_index("docs"), 2)

    def place(index, piece):
        start = pl.multiple_of(index * tokens, BLOCK)
        keys[pl.ds(start, tokens), :] = piece[0]
        values[pl.ds(start, tokens), :HD] = piece[1]

    values[:, HD:] = jnp.ones((values.shape[0], HD), values.dtype)
    place(0 + odd, far)
    place(1 - odd, far_other)
    place(2 + odd, near)
    place(3 - odd, near_other)
    place(4 + odd, own)
    place(5 - odd, other)


def prepare(pieces):
    rows = len(pieces) * pieces[0].shape[1]
    return pl.pallas_call(
        gather_rows,
        out_shape=(
            jax.ShapeDtypeStruct((rows, HD), jnp.bfloat16),
            jax.ShapeDtypeStruct((rows, 2 * HD), jnp.bfloat16),
        ),
        in_specs=[VMEM] * len(pieces),
        out_specs=(VMEM, VMEM),
        compiler_params=pltpu.CompilerParams(vmem_limit_bytes=12 << 20),
        name="prepare",
    )(*pieces)


def attend(docs, query, keys, values, out, stacked, scores, peak, total, *, first, blocks):
    heads = query.shape[1] // HD
    span = STEP * BLOCK
    shard = lax.axis_index("docs")
    local_blocks = keys.shape[0] // 6 // BLOCK
    odd = lax.rem(shard, 2)

    def one_block(row):
        place_in = shard * local_blocks + first + row
        begin = jnp.int32(0)
        edge = jnp.int32(0)
        for doc in range(docs.shape[0]):
            edge = edge + docs[doc]
            begin = jnp.where(edge <= place_in, edge, begin)
        count = place_in - begin + 1
        steps = lax.div(count + STEP - 1, STEP)
        last = (4 + odd) * local_blocks + first + row
        here_row = pl.multiple_of(row * BLOCK, BLOCK)
        for head in range(heads):
            stacked[head * BLOCK : (head + 1) * BLOCK, :] = query[
                pl.ds(here_row, BLOCK), head * HD : (head + 1) * HD
            ]

        def score(step, masked):
            start = pl.multiple_of((last - step * STEP - (STEP - 1)) * BLOCK, BLOCK)
            part = keys[pl.ds(start, span), :]
            column = pl.multiple_of(step * span, span)
            for head in range(heads):
                here = slice(head * BLOCK, (head + 1) * BLOCK)
                got = lax.dot_general(
                    stacked[here, :], part, (((1,), (1,)), ((), ())),
                    preferred_element_type=jnp.float32,
                )
                high = None
                for block in range(STEP):
                    piece = got[:, block * BLOCK : (block + 1) * BLOCK]
                    if masked:
                        back = step * STEP + (STEP - 1 - block)
                        keep = jnp.broadcast_to(back < count, piece.shape)
                        if block == STEP - 1:
                            down = lax.broadcasted_iota(jnp.int32, piece.shape, 0)
                            across = lax.broadcasted_iota(jnp.int32, piece.shape, 1)
                            keep = keep & ((across <= down) | (step > 0))
                        piece = jnp.where(keep, piece, MASKED)
                    scores[here, pl.ds(pl.multiple_of(column + block * BLOCK, BLOCK), BLOCK)] = piece
                    high = piece if high is None else jnp.maximum(high, piece)
                peak[here, :] = jnp.maximum(peak[here, :], high)

        peak[...] = jnp.full(peak.shape, MASKED, jnp.float32)
        score(jnp.int32(0), True)

        def middle(step, carry):
            score(step, False)
            return carry

        lax.fori_loop(1, steps - 1, middle, 0)

        @pl.when(steps > 1)
        def _():
            score(steps - 1, True)

        for head in range(heads):
            here = slice(head * BLOCK, (head + 1) * BLOCK)
            peak[here, :] = jnp.broadcast_to(
                jnp.max(peak[here, :], axis=1, keepdims=True), (BLOCK, BLOCK)
            )
        total[...] = jnp.zeros(total.shape, jnp.float32)

        def weigh(step, carry):
            start = pl.multiple_of((last - step * STEP - (STEP - 1)) * BLOCK, BLOCK)
            part = values[pl.ds(start, span), :]
            column = pl.multiple_of(step * span, span)
            for head in range(heads):
                here = slice(head * BLOCK, (head + 1) * BLOCK)
                top = jnp.concatenate([peak[here, :]] * STEP, axis=1)
                raised = jnp.exp2((scores[here, pl.ds(column, span)] - top) * EXP2_SCALE)
                total[here, :] += jnp.dot(
                    raised.astype(jnp.bfloat16), part, preferred_element_type=jnp.float32
                )
            return carry

        lax.fori_loop(0, steps, weigh, 0)
        for head in range(heads):
            here = slice(head * BLOCK, (head + 1) * BLOCK)
            out[pl.ds(here_row, BLOCK), head * HD : (head + 1) * HD] = (
                total[here, :HD] / total[here, HD:]
            ).astype(out.dtype)

    for row in range(blocks):
        one_block(row)


def attention(docs, query, keys, values, part, blocks):
    width = query.shape[1]
    rows = width // HD * BLOCK
    return pl.pallas_call(
        functools.partial(attend, first=part * blocks, blocks=blocks),
        out_shape=jax.ShapeDtypeStruct((blocks * BLOCK, width), jnp.bfloat16),
        grid=(1,),
        in_specs=[SMEM, pl.BlockSpec((blocks * BLOCK, width), lambda i: (part, 0)), VMEM, VMEM],
        out_specs=VMEM,
        scratch_shapes=[
            pltpu.VMEM((rows, HD), jnp.bfloat16),
            pltpu.VMEM((rows, MOSTB * BLOCK), jnp.float32),
            pltpu.VMEM((rows, BLOCK), jnp.float32),
            pltpu.VMEM((rows, 2 * HD), jnp.float32),
        ],
        compiler_params=pltpu.CompilerParams(vmem_limit_bytes=24 << 20),
        name="attend",
    )(docs, query, keys, values)


def project(parts, pieces, half):
    part_tokens, depth = parts[0].shape
    tokens = part_tokens * len(parts)
    width = pieces[0].shape[1]
    slots = 4

    def body(*refs):
        lefts, refs = refs[: len(parts)], refs[len(parts) :]
        sources = refs[: len(pieces)]
        outs = refs[len(pieces) : len(pieces) + 2]
        rights, sems = refs[len(pieces) + 2 :]
        shard = lax.axis_index("docs")
        group = lax.axis_index("heads")
        odd = lax.rem(shard, 2)
        plane = lax.div(shard, 2)
        early = jnp.where(odd == 1, 2, 1)
        late = 3 - early
        targets = [group ^ early, group ^ 3, group, group ^ late]
        for slot, target in enumerate(targets):
            distance = jnp.abs(plane - target)
            below = jnp.where(target < plane, 1, 0)
            away = 2 * distance + (below ^ odd)
            index = jnp.where(distance == 0, odd ^ half, away)
            for j, source in enumerate(sources):
                @pl.when(index == j)
                def _(source=source, slot=slot):
                    pltpu.make_async_copy(source, rights.at[slot], sems.at[slot]).start()
        for slot in range(slots):
            pltpu.make_async_copy(sources[0], rights.at[slot], sems.at[slot]).wait()
            for part, left in enumerate(lefts):
                outs[slot // 2][slot % 2, part * part_tokens : (part + 1) * part_tokens, :] = jnp.dot(
                    left[...], rights[slot], preferred_element_type=jnp.float32
                ).astype(jnp.bfloat16)

    shape = jax.ShapeDtypeStruct((2, tokens, width), jnp.bfloat16)
    return pl.pallas_call(
        body,
        out_shape=(shape, shape),
        in_specs=[VMEM] * len(parts) + [ANY] * len(pieces),
        out_specs=(VMEM, VMEM),
        scratch_shapes=[pltpu.VMEM((slots, depth, width), jnp.bfloat16), pltpu.SemaphoreType.DMA((slots,))],
        compiler_params=pltpu.CompilerParams(vmem_limit_bytes=16 << 20),
        name="project",
    )(*parts, *pieces)


def build(shards, groups):
    def send(block, route, axis="docs"):
        return lax.ppermute(block, axis, route)

    swap = [(i, i ^ 1) for i in range(shards)]
    up = [(i, i + 2) for i in range(shards - 2)]
    cross = []
    for i in range(0, shards - 2, 2):
        cross += [(i, i + 3), (i + 3, i)]

    def exchange(block, early):
        route = []
        for group in range(groups):
            for shard in range(shards):
                flip = 1 if (shard % 2 == 0) == early else 2
                route.append((group * shards + shard, (group ^ flip) * shards + shard))
        return send(block, route, ("heads", "docs"))

    def local(query_rows, key_rows, value_rows, doc_blocks, out_weight):
        return inside(query_rows, key_rows, value_rows, doc_blocks, out_weight)

    def inside(query_rows, key_rows, value_rows, doc_blocks, out_weight):
        f32 = jnp.float32
        own = jnp.stack([key_rows, value_rows])
        other = send(own, swap)
        near = send(own, up)
        near_other = send(near, swap)
        far = send(near, up)
        far_other = send(far, swap)
        keys, values = prepare((own, other, near, near_other, far, far_other))
        blocks = own.shape[1] // BLOCK // PARTS
        attended = []
        for part in range(PARTS):
            attended.append(attention(doc_blocks, query_rows, keys, values, part, blocks))

        if shards != 2 * groups:
            weight = lax.all_gather(out_weight, "docs", axis=1, tiled=True)
            partial = jnp.dot(jnp.concatenate(attended), weight, preferred_element_type=f32)
            return lax.psum_scatter(
                partial.astype(jnp.bfloat16), "heads", scatter_dimension=1, tiled=True
            )

        weight_other = send(out_weight, swap)
        pieces = []
        for last in (out_weight, weight_other):
            found = [out_weight, weight_other]
            for _ in range(1, shards // 2):
                got = send(last, cross)
                last = send(got, swap)
                found += [got, last]
            pieces.append(found)
        results = []
        for half in range(2):
            outward, keep = project(attended, pieces[half], half)
            arrived = exchange(outward, True)
            onward = (keep[1].astype(f32) + arrived[1].astype(f32)).astype(jnp.bfloat16)
            final = exchange(onward, False)
            results.append((keep[0].astype(f32) + arrived[0].astype(f32) + final.astype(f32)).astype(jnp.bfloat16))
        ahead = lax.axis_index("heads") > lax.axis_index("docs") // 2
        return jnp.concatenate(
            [jnp.where(ahead, results[1], results[0]), jnp.where(ahead, results[0], results[1])], axis=1
        )

    return local


PARTS = 4


def solution(mesh):
    placed = (P("docs", "heads"), P("docs", "heads"), P("docs", "heads"), P(), P("heads", "docs"))
    shards, groups = mesh.shape["docs"], mesh.shape["heads"]
    return jax.shard_map(
        build(shards, groups), mesh=mesh, in_specs=placed, out_specs=P("docs", "heads"), check_vma=False
    )
```

time: 118 us -> 115 us (0.975)
  the two profiles are of different devices: /device:TPU:16 before, /device:TPU:9 now
where the time goes in v2:
time: 115 us
  waiting for transfers between devices  47.2 us (41%)
  starting transfers between devices  40.5 us (35%)
  Pallas kernels  24.8 us (22%)
  other arithmetic  2.18 us (2%)
    ppermute x22, waiting for transfers between devices, send(): return lax.ppermute(block, axis, route)  47.2 us
    ppermute x22, starting transfers between devices, send(): return lax.ppermute(block, axis, route)  40.5 us
    pallas_call x4, Pallas kernels, attention(): pl.pallas_call(functools.partial(attend, first=part * blocks, blocks=bloc...  20.1 us
    pallas_call x2, Pallas kernels, project(): pl.pallas_call(body, out_shape=(shape, shape), in_specs=[VMEM] * len(part...  4.39 us
  transfers between devices with their start and end apart: 22, of which 9 were waited for; matrix products, arithmetic and copies ran while one was open for 1% of the time, Pallas kernels for 22%

profile of v2, /device:TPU:9, one launch (start us, length us, event | category | flops | bytes accessed | tf_op | source)
XLA Modules:
  0.0 114.8 jit_solution(15442693517602139785)
XLA Ops:
  0.7 1.9 %collective-permute-start.14 = (bf16[1024,256]{1,0:T(8,128)(2,1)}, bf16[1024,256]{1,0:T(8,128)(2,1)S(1)}, u32[]{:S(2)}, u32[]{:S(2)}) collective-permute-start(bf16[1024,256]{1,0:T(8,128)(2,1)} %refs_4_.3), channel_id=1, source_target_pairs={{0,3},{3,0},{2,5},{5,2},{4,7},{7,4},{8,11},{11,8},{10,13},{13,10},... | collective-permute-start | bytes 1572872 | tf_op jit(solution)/shard_map/ppermute | solution.py:213
  2.6 3.6 %collective-permute-start.6 = (bf16[1024,256]{1,0:T(8,128)(2,1)S(1)}, bf16[1024,256]{1,0:T(8,128)(2,1)S(1)}, u32[]{:S(2)}, u32[]{:S(2)}) collective-permute-start(bf16[1024,256]{1,0:T(8,128)(2,1)S(1)} %collective-permute-done.5.refs_5_), channel_id=1, source_target_pairs={{0,3},{3,0},{2,5},{5,2},{4,7},{7,4},{8,11},{11,8},{10,13},{13,10},... | collective-permute-start | bytes 1572872 | tf_op jit(solution)/shard_map/ppermute | solution.py:213
  6.3 5.4 %collective-permute-done.14.refs_6_ = bf16[1024,256]{1,0:T(8,128)(2,1)S(1)} collective-permute-done((bf16[1024,256]{1,0:T(8,128)(2,1)}, bf16[1024,256]{1,0:T(8,128)(2,1)S(1)}, u32[]{:S(2)}, u32[]{:S(2)}) %collective-permute-start.14) | collective-permute-done | bytes 524320 | tf_op jit(solution)/shard_map/ppermute | solution.py:213
  11.7 5.3 %collective-permute-done.6.refs_6_ = bf16[1024,256]{1,0:T(8,128)(2,1)S(1)} collective-permute-done((bf16[1024,256]{1,0:T(8,128)(2,1)S(1)}, bf16[1024,256]{1,0:T(8,128)(2,1)S(1)}, u32[]{:S(2)}, u32[]{:S(2)}) %collective-permute-start.6) | collective-permute-done | bytes 524320 | tf_op jit(solution)/shard_map/ppermute | solution.py:213
  17.2 1.9 %collective-permute-start.16 = (bf16[1024,256]{1,0:T(8,128)(2,1)S(1)}, bf16[1024,256]{1,0:T(8,128)(2,1)S(1)}, u32[]{:S(2)}, u32[]{:S(2)}) collective-permute-start(bf16[1024,256]{1,0:T(8,128)(2,1)S(1)} %collective-permute-done.15.refs_7_), channel_id=1, source_target_pairs={{0,3},{3,0},{2,5},{5,2},{4,7},{7,4},{8,11},{11,8},{10,13},{13,10},... | collective-permute-start | bytes 1572872 | tf_op jit(solution)/shard_map/ppermute | solution.py:213
  19.1 3.6 %collective-permute-start.8 = (bf16[1024,256]{1,0:T(8,128)(2,1)S(1)}, bf16[1024,256]{1,0:T(8,128)(2,1)S(1)}, u32[]{:S(2)}, u32[]{:S(2)}) collective-permute-start(bf16[1024,256]{1,0:T(8,128)(2,1)S(1)} %collective-permute-done.7.refs_7_), channel_id=1, source_target_pairs={{0,3},{3,0},{2,5},{5,2},{4,7},{7,4},{8,11},{11,8},{10,13},{13,10},... | collective-permute-start | bytes 1572872 | tf_op jit(solution)/shard_map/ppermute | solution.py:213
  22.7 5.2 %collective-permute-done.16.refs_8_ = bf16[1024,256]{1,0:T(8,128)(2,1)S(1)} collective-permute-done((bf16[1024,256]{1,0:T(8,128)(2,1)S(1)}, bf16[1024,256]{1,0:T(8,128)(2,1)S(1)}, u32[]{:S(2)}, u32[]{:S(2)}) %collective-permute-start.16) | collective-permute-done | bytes 524320 | tf_op jit(solution)/shard_map/ppermute | solution.py:213
  28.0 5.3 %collective-permute-done.8.refs_8_ = bf16[1024,256]{1,0:T(8,128)(2,1)S(1)} collective-permute-done((bf16[1024,256]{1,0:T(8,128)(2,1)S(1)}, bf16[1024,256]{1,0:T(8,128)(2,1)S(1)}, u32[]{:S(2)}, u32[]{:S(2)}) %collective-permute-start.8) | collective-permute-done | bytes 524320 | tf_op jit(solution)/shard_map/ppermute | solution.py:213
  33.6 1.9 %collective-permute-start.18 = (bf16[1024,256]{1,0:T(8,128)(2,1)S(1)}, bf16[1024,256]{1,0:T(8,128)(2,1)S(1)}, u32[]{:S(2)}, u32[]{:S(2)}) collective-permute-start(bf16[1024,256]{1,0:T(8,128)(2,1)S(1)} %collective-permute-done.17.refs_9_), channel_id=1, source_target_pairs={{0,3},{3,0},{2,5},{5,2},{4,7},{7,4},{8,11},{11,8},{10,13},{13,10},... | collective-permute-start | bytes 1572872 | tf_op jit(solution)/shard_map/ppermute | solution.py:213
  35.6 3.6 %collective-permute-start.10 = (bf16[1024,256]{1,0:T(8,128)(2,1)S(1)}, bf16[1024,256]{1,0:T(8,128)(2,1)S(1)}, u32[]{:S(2)}, u32[]{:S(2)}) collective-permute-start(bf16[1024,256]{1,0:T(8,128)(2,1)S(1)} %collective-permute-done.9.refs_9_), channel_id=1, source_target_pairs={{0,3},{3,0},{2,5},{5,2},{4,7},{7,4},{8,11},{11,8},{10,13},{13,10},... | collective-permute-start | bytes 1572872 | tf_op jit(solution)/shard_map/ppermute | solution.py:213
  40.2 3.2 %collective-permute-start.1 = (bf16[2,512,128]{2,1,0:T(8,128)(2,1)S(1)}, bf16[2,512,128]{2,1,0:T(8,128)(2,1)S(1)}, u32[]{:S(2)}, u32[]{:S(2)}) collective-permute-start(bf16[2,512,128]{2,1,0:T(8,128)(2,1)S(1)} %pad_maximum_fusion.1.own), channel_id=1, source_target_pairs={{0,2},{1,3},{2,4},{3,5},{4,6},{5,7},{8,10},{9,11},{10,12},{11,13},... | collective-permute-start | bytes 786440 | tf_op jit(solution)/shard_map/ppermute | solution.py:213
  43.4 6.7 %collective-permute-done.1.near = bf16[2,512,128]{2,1,0:T(8,128)(2,1)S(1)} collective-permute-done((bf16[2,512,128]{2,1,0:T(8,128)(2,1)S(1)}, bf16[2,512,128]{2,1,0:T(8,128)(2,1)S(1)}, u32[]{:S(2)}, u32[]{:S(2)}) %collective-permute-start.1) | collective-permute-done | bytes 262176 | tf_op jit(solution)/shard_map/ppermute | solution.py:213
  50.1 3.2 %collective-permute-start.3 = (bf16[2,512,128]{2,1,0:T(8,128)(2,1)S(1)}, bf16[2,512,128]{2,1,0:T(8,128)(2,1)S(1)}, u32[]{:S(2)}, u32[]{:S(2)}) collective-permute-start(bf16[2,512,128]{2,1,0:T(8,128)(2,1)S(1)} %collective-permute-done.1.near), channel_id=1, source_target_pairs={{0,2},{1,3},{2,4},{3,5},{4,6},{5,7},{8,10},{9,11},{10,12},{11,13},... | collective-permute-start | bytes 786440 | tf_op jit(solution)/shard_map/ppermute | solution.py:213
  53.3 7.2 %collective-permute-start.19 = (bf16[1024,256]{1,0:T(8,128)(2,1)S(1)}, bf16[1024,256]{1,0:T(8,128)(2,1)S(1)}, u32[]{:S(2)}, u32[]{:S(2)}) collective-permute-start(bf16[1024,256]{1,0:T(8,128)(2,1)S(1)} %collective-permute-done.18.refs_10_), channel_id=1, source_target_pairs={{0,1},{1,0},{2,3},{3,2},{4,5},{5,4},{6,7},{7,6},{8,9},{9,8},{10,11... | collective-permute-start | bytes 1572872 | tf_op jit(solution)/shard_map/ppermute | solution.py:213
  61.1 4.1 %collective-permute-start.4 = (bf16[2,512,128]{2,1,0:T(8,128)(2,1)S(1)}, bf16[2,512,128]{2,1,0:T(8,128)(2,1)S(1)}, u32[]{:S(2)}, u32[]{:S(2)}) collective-permute-start(bf16[2,512,128]{2,1,0:T(8,128)(2,1)S(1)} %collective-permute-done.3.far), channel_id=1, source_target_pairs={{0,1},{1,0},{2,3},{3,2},{4,5},{5,4},{6,7},{7,6},{8,9},{9,8},{10,11... | collective-permute-start | bytes 786440 | tf_op jit(solution)/shard_map/ppermute | solution.py:213
  66.7 5.0 %attend.7.refs_3_ = bf16[128,1024]{1,0:T(8,128)(2,1)S(1)} custom-call(s32[4]{0:T(128)S(1)} %copy-done.2, bf16[512,1024]{1,0:T(8,128)(2,1)S(1)} %copy-done, bf16[3072,128]{1,0:T(8,128)(2,1)S(1)} %get-tuple-element.11.keys, bf16[3072,256]{1,0:T(8,128)(2,1)S(1)} %get-tuple-element.12.values), custom_call_target="tpu_custom_call" | custom-call | tf_op jit(solution)/shard_map/attend/pallas_call | solution.py:148
  71.7 5.0 %attend.6.refs_2_ = bf16[128,1024]{1,0:T(8,128)(2,1)S(1)} custom-call(s32[4]{0:T(128)S(1)} %copy-done.2, bf16[512,1024]{1,0:T(8,128)(2,1)S(1)} %copy-done, bf16[3072,128]{1,0:T(8,128)(2,1)S(1)} %get-tuple-element.11.keys, bf16[3072,256]{1,0:T(8,128)(2,1)S(1)} %get-tuple-element.12.values), custom_call_target="tpu_custom_call" | custom-call | tf_op jit(solution)/shard_map/attend/pallas_call | solution.py:148
  76.8 5.0 %attend.5.refs_1_ = bf16[128,1024]{1,0:T(8,128)(2,1)S(1)} custom-call(s32[4]{0:T(128)S(1)} %copy-done.2, bf16[512,1024]{1,0:T(8,128)(2,1)S(1)} %copy-done, bf16[3072,128]{1,0:T(8,128)(2,1)S(1)} %get-tuple-element.11.keys, bf16[3072,256]{1,0:T(8,128)(2,1)S(1)} %get-tuple-element.12.values), custom_call_target="tpu_custom_call" | custom-call | tf_op jit(solution)/shard_map/attend/pallas_call | solution.py:148
  81.8 5.0 %attend.4.refs_0_ = bf16[128,1024]{1,0:T(8,128)(2,1)S(1)} custom-call(s32[4]{0:T(128)S(1)} %copy-done.2, bf16[512,1024]{1,0:T(8,128)(2,1)S(1)} %copy-done, bf16[3072,128]{1,0:T(8,128)(2,1)S(1)} %get-tuple-element.11.keys, bf16[3072,256]{1,0:T(8,128)(2,1)S(1)} %get-tuple-element.12.values), custom_call_target="tpu_custom_call" | custom-call | tf_op jit(solution)/shard_map/attend/pallas_call | solution.py:148
  86.8 2.2 %project.3 = (bf16[2,512,256]{2,1,0:T(8,128)(2,1)S(1)}, bf16[2,512,256]{2,1,0:T(8,128)(2,1)S(1)}) custom-call(bf16[128,1024]{1,0:T(8,128)(2,1)S(1)} %attend.4.refs_0_, bf16[128,1024]{1,0:T(8,128)(2,1)S(1)} %attend.5.refs_1_, bf16[128,1024]{1,0:T(8,128)(2,1)S(1)} %attend.6.refs_2_, bf16[128,1024]{1,0:T(8,128)(2,1)S(1)} %attend.7.refs_3_, ...), custom_call_target="tpu_custom_call" | custom-call | tf_op jit(solution)/shard_map/project/pallas_call | solution.py:200
  90.4 2.2 %project.2 = (bf16[2,512,256]{2,1,0:T(8,128)(2,1)S(1)}, bf16[2,512,256]{2,1,0:T(8,128)(2,1)S(1)}) custom-call(bf16[128,1024]{1,0:T(8,128)(2,1)S(1)} %attend.4.refs_0_, bf16[128,1024]{1,0:T(8,128)(2,1)S(1)} %attend.5.refs_1_, bf16[128,1024]{1,0:T(8,128)(2,1)S(1)} %attend.6.refs_2_, bf16[128,1024]{1,0:T(8,128)(2,1)S(1)} %attend.7.refs_3_, ...), custom_call_target="tpu_custom_call" | custom-call | tf_op jit(solution)/shard_map/project/pallas_call | solution.py:200
  93.0 4.4 %collective-permute-done.20 = bf16[2,512,256]{2,1,0:T(8,128)(2,1)S(1)} collective-permute-done((bf16[2,512,256]{2,1,0:T(8,128)(2,1)S(1)}, bf16[2,512,256]{2,1,0:T(8,128)(2,1)S(1)}, u32[]{:S(2)}, u32[]{:S(2)}) %collective-permute-start.20) | collective-permute-done | bytes 524320 | tf_op jit(solution)/shard_map/ppermute | solution.py:213
  98.8 9.6 %collective-permute-done.12 = bf16[2,512,256]{2,1,0:T(8,128)(2,1)S(1)} collective-permute-done((bf16[2,512,256]{2,1,0:T(8,128)(2,1)S(1)}, bf16[2,512,256]{2,1,0:T(8,128)(2,1)S(1)}, u32[]{:S(2)}, u32[]{:S(2)}) %collective-permute-start.12) | collective-permute-done | bytes 524320 | tf_op jit(solution)/shard_map/ppermute | solution.py:213
  109.7 4.0 %collective-permute-done.13 = bf16[512,256]{1,0:T(8,128)(2,1)S(1)} collective-permute-done((bf16[512,256]{1,0:T(8,128)(2,1)S(1)}, bf16[512,256]{1,0:T(8,128)(2,1)S(1)}, u32[]{:S(2)}, u32[]{:S(2)}) %collective-permute-start.13) | collective-permute-done | bytes 262176 | tf_op jit(solution)/shard_map/ppermute | solution.py:213
  (38 shorter events, 9.8 us)
Async XLA Ops:
  0.0 66.7 %copy-start = (bf16[512,1024]{1,0:T(8,128)(2,1)S(1)}, bf16[512,1024]{1,0:T(8,128)(2,1)}, u32[]{:S(2)}) copy-start(bf16[512,1024]{1,0:T(8,128)(2,1)} %query.7) | copy-start | bytes 3145732
  0.0 66.7 %copy-start.2 = (s32[4]{0:T(128)S(1)}, s32[4]{0:T(128)}, u32[]{:S(2)}) copy-start(s32[4]{0:T(128)} %docs.7) | copy-start | bytes 52
  0.0 2.6 %collective-permute-start.5 = (bf16[1024,256]{1,0:T(8,128)(2,1)}, bf16[1024,256]{1,0:T(8,128)(2,1)S(1)}, u32[]{:S(2)}, u32[]{:S(2)}) collective-permute-start(bf16[1024,256]{1,0:T(8,128)(2,1)} %refs_4_.3), channel_id=1, source_target_pairs={{0,1},{1,0},{2,3},{3,2},{4,5},{5,4},{6,7},{7,6},{8,9},{9,8},{10,11... | collective-permute-start | bytes 1572872 | tf_op jit(solution)/shard_map/ppermute | solution.py:213
  0.7 11.0 %collective-permute-start.14 = (bf16[1024,256]{1,0:T(8,128)(2,1)}, bf16[1024,256]{1,0:T(8,128)(2,1)S(1)}, u32[]{:S(2)}, u32[]{:S(2)}) collective-permute-start(bf16[1024,256]{1,0:T(8,128)(2,1)} %refs_4_.3), channel_id=1, source_target_pairs={{0,3},{3,0},{2,5},{5,2},{4,7},{7,4},{8,11},{11,8},{10,13},{13,10},... | collective-permute-start | bytes 1572872 | tf_op jit(solution)/shard_map/ppermute | solution.py:213
  2.6 14.4 %collective-permute-start.6 = (bf16[1024,256]{1,0:T(8,128)(2,1)S(1)}, bf16[1024,256]{1,0:T(8,128)(2,1)S(1)}, u32[]{:S(2)}, u32[]{:S(2)}) collective-permute-start(bf16[1024,256]{1,0:T(8,128)(2,1)S(1)} %collective-permute-done.5.refs_5_), channel_id=1, source_target_pairs={{0,3},{3,0},{2,5},{5,2},{4,7},{7,4},{8,11},{11,8},{10,13},{13,10},... | collective-permute-start | bytes 1572872 | tf_op jit(solution)/shard_map/ppermute | solution.py:213
  11.7 5.5 %collective-permute-start.15 = (bf16[1024,256]{1,0:T(8,128)(2,1)S(1)}, bf16[1024,256]{1,0:T(8,128)(2,1)S(1)}, u32[]{:S(2)}, u32[]{:S(2)}) collective-permute-start(bf16[1024,256]{1,0:T(8,128)(2,1)S(1)} %collective-permute-done.14.refs_6_), channel_id=1, source_target_pairs={{0,1},{1,0},{2,3},{3,2},{4,5},{5,4},{6,7},{7,6},{8,9},{9,8},{10,11... | collective-permute-start | bytes 1572872 | tf_op jit(solution)/shard_map/ppermute | solution.py:213
  17.0 2.1 %collective-permute-start.7 = (bf16[1024,256]{1,0:T(8,128)(2,1)S(1)}, bf16[1024,256]{1,0:T(8,128)(2,1)S(1)}, u32[]{:S(2)}, u32[]{:S(2)}) collective-permute-start(bf16[1024,256]{1,0:T(8,128)(2,1)S(1)} %collective-permute-done.6.refs_6_), channel_id=1, source_target_pairs={{0,1},{1,0},{2,3},{3,2},{4,5},{5,4},{6,7},{7,6},{8,9},{9,8},{10,11... | collective-permute-start | bytes 1572872 | tf_op jit(solution)/shard_map/ppermute | solution.py:213
  17.2 10.8 %collective-permute-start.16 = (bf16[1024,256]{1,0:T(8,128)(2,1)S(1)}, bf16[1024,256]{1,0:T(8,128)(2,1)S(1)}, u32[]{:S(2)}, u32[]{:S(2)}) collective-permute-start(bf16[1024,256]{1,0:T(8,128)(2,1)S(1)} %collective-permute-done.15.refs_7_), channel_id=1, source_target_pairs={{0,3},{3,0},{2,5},{5,2},{4,7},{7,4},{8,11},{11,8},{10,13},{13,10},... | collective-permute-start | bytes 1572872 | tf_op jit(solution)/shard_map/ppermute | solution.py:213
  19.1 14.2 %collective-permute-start.8 = (bf16[1024,256]{1,0:T(8,128)(2,1)S(1)}, bf16[1024,256]{1,0:T(8,128)(2,1)S(1)}, u32[]{:S(2)}, u32[]{:S(2)}) collective-permute-start(bf16[1024,256]{1,0:T(8,128)(2,1)S(1)} %collective-permute-done.7.refs_7_), channel_id=1, source_target_pairs={{0,3},{3,0},{2,5},{5,2},{4,7},{7,4},{8,11},{11,8},{10,13},{13,10},... | collective-permute-start | bytes 1572872 | tf_op jit(solution)/shard_map/ppermute | solution.py:213
  27.9 5.7 %collective-permute-start.17 = (bf16[1024,256]{1,0:T(8,128)(2,1)S(1)}, bf16[1024,256]{1,0:T(8,128)(2,1)S(1)}, u32[]{:S(2)}, u32[]{:S(2)}) collective-permute-start(bf16[1024,256]{1,0:T(8,128)(2,1)S(1)} %collective-permute-done.16.refs_8_), channel_id=1, source_target_pairs={{0,1},{1,0},{2,3},{3,2},{4,5},{5,4},{6,7},{7,6},{8,9},{9,8},{10,11... | collective-permute-start | bytes 1572872 | tf_op jit(solution)/shard_map/ppermute | solution.py:213
  33.3 2.3 %collective-permute-start.9 = (bf16[1024,256]{1,0:T(8,128)(2,1)S(1)}, bf16[1024,256]{1,0:T(8,128)(2,1)S(1)}, u32[]{:S(2)}, u32[]{:S(2)}) collective-permute-start(bf16[1024,256]{1,0:T(8,128)(2,1)S(1)} %collective-permute-done.8.refs_8_), channel_id=1, source_target_pairs={{0,1},{1,0},{2,3},{3,2},{4,5},{5,4},{6,7},{7,6},{8,9},{9,8},{10,11... | collective-permute-start | bytes 1572872 | tf_op jit(solution)/shard_map/ppermute | solution.py:213
  33.6 19.7 %collective-permute-start.18 = (bf16[1024,256]{1,0:T(8,128)(2,1)S(1)}, bf16[1024,256]{1,0:T(8,128)(2,1)S(1)}, u32[]{:S(2)}, u32[]{:S(2)}) collective-permute-start(bf16[1024,256]{1,0:T(8,128)(2,1)S(1)} %collective-permute-done.17.refs_9_), channel_id=1, source_target_pairs={{0,3},{3,0},{2,5},{5,2},{4,7},{7,4},{8,11},{11,8},{10,13},{13,10},... | collective-permute-start | bytes 1572872 | tf_op jit(solution)/shard_map/ppermute | solution.py:213
  35.6 25.0 %collective-permute-start.10 = (bf16[1024,256]{1,0:T(8,128)(2,1)S(1)}, bf16[1024,256]{1,0:T(8,128)(2,1)S(1)}, u32[]{:S(2)}, u32[]{:S(2)}) collective-permute-start(bf16[1024,256]{1,0:T(8,128)(2,1)S(1)} %collective-permute-done.9.refs_9_), channel_id=1, source_target_pairs={{0,3},{3,0},{2,5},{5,2},{4,7},{7,4},{8,11},{11,8},{10,13},{13,10},... | collective-permute-start | bytes 1572872 | tf_op jit(solution)/shard_map/ppermute | solution.py:213
  40.2 9.9 %collective-permute-start.1 = (bf16[2,512,128]{2,1,0:T(8,128)(2,1)S(1)}, bf16[2,512,128]{2,1,0:T(8,128)(2,1)S(1)}, u32[]{:S(2)}, u32[]{:S(2)}) collective-permute-start(bf16[2,512,128]{2,1,0:T(8,128)(2,1)S(1)} %pad_maximum_fusion.1.own), channel_id=1, source_target_pairs={{0,2},{1,3},{2,4},{3,5},{4,6},{5,7},{8,10},{9,11},{10,12},{11,13},... | collective-permute-start | bytes 786440 | tf_op jit(solution)/shard_map/ppermute | solution.py:213
  50.1 11.0 %collective-permute-start.3 = (bf16[2,512,128]{2,1,0:T(8,128)(2,1)S(1)}, bf16[2,512,128]{2,1,0:T(8,128)(2,1)S(1)}, u32[]{:S(2)}, u32[]{:S(2)}) collective-permute-start(bf16[2,512,128]{2,1,0:T(8,128)(2,1)S(1)} %collective-permute-done.1.near), channel_id=1, source_target_pairs={{0,2},{1,3},{2,4},{3,5},{4,6},{5,7},{8,10},{9,11},{10,12},{11,13},... | collective-permute-start | bytes 786440 | tf_op jit(solution)/shard_map/ppermute | solution.py:213
  53.3 33.5 %collective-permute-start.19 = (bf16[1024,256]{1,0:T(8,128)(2,1)S(1)}, bf16[1024,256]{1,0:T(8,128)(2,1)S(1)}, u32[]{:S(2)}, u32[]{:S(2)}) collective-permute-start(bf16[1024,256]{1,0:T(8,128)(2,1)S(1)} %collective-permute-done.18.refs_10_), channel_id=1, source_target_pairs={{0,1},{1,0},{2,3},{3,2},{4,5},{5,4},{6,7},{7,6},{8,9},{9,8},{10,11... | collective-permute-start | bytes 1572872 | tf_op jit(solution)/shard_map/ppermute | solution.py:213
  60.5 29.8 %collective-permute-start.11 = (bf16[1024,256]{1,0:T(8,128)(2,1)S(1)}, bf16[1024,256]{1,0:T(8,128)(2,1)S(1)}, u32[]{:S(2)}, u32[]{:S(2)}) collective-permute-start(bf16[1024,256]{1,0:T(8,128)(2,1)S(1)} %collective-permute-done.10.refs_10_), channel_id=1, source_target_pairs={{0,1},{1,0},{2,3},{3,2},{4,5},{5,4},{6,7},{7,6},{8,9},{9,8},{10,11... | collective-permute-start | bytes 1572872 | tf_op jit(solution)/shard_map/ppermute | solution.py:213
  60.6 4.6 %collective-permute-start = (bf16[2,512,128]{2,1,0:T(8,128)(2,1)S(1)}, bf16[2,512,128]{2,1,0:T(8,128)(2,1)S(1)}, u32[]{:S(2)}, u32[]{:S(2)}) collective-permute-start(bf16[2,512,128]{2,1,0:T(8,128)(2,1)S(1)} %pad_maximum_fusion.1.own), channel_id=1, source_target_pairs={{0,1},{1,0},{2,3},{3,2},{4,5},{5,4},{6,7},{7,6},{8,9},{9,8},{10,11... | collective-permute-start | bytes 786440 | tf_op jit(solution)/shard_map/ppermute | solution.py:213
  61.0 4.2 %collective-permute-start.2 = (bf16[2,512,128]{2,1,0:T(8,128)(2,1)S(1)}, bf16[2,512,128]{2,1,0:T(8,128)(2,1)S(1)}, u32[]{:S(2)}, u32[]{:S(2)}) collective-permute-start(bf16[2,512,128]{2,1,0:T(8,128)(2,1)S(1)} %collective-permute-done.1.near), channel_id=1, source_target_pairs={{0,1},{1,0},{2,3},{3,2},{4,5},{5,4},{6,7},{7,6},{8,9},{9,8},{10,11... | collective-permute-start | bytes 786440 | tf_op jit(solution)/shard_map/ppermute | solution.py:213
  61.1 5.3 %collective-permute-start.4 = (bf16[2,512,128]{2,1,0:T(8,128)(2,1)S(1)}, bf16[2,512,128]{2,1,0:T(8,128)(2,1)S(1)}, u32[]{:S(2)}, u32[]{:S(2)}) collective-permute-start(bf16[2,512,128]{2,1,0:T(8,128)(2,1)S(1)} %collective-permute-done.3.far), channel_id=1, source_target_pairs={{0,1},{1,0},{2,3},{3,2},{4,5},{5,4},{6,7},{7,6},{8,9},{9,8},{10,11... | collective-permute-start | bytes 786440 | tf_op jit(solution)/shard_map/ppermute | solution.py:213
  89.1 8.4 %collective-permute-start.20 = (bf16[2,512,256]{2,1,0:T(8,128)(2,1)S(1)}, bf16[2,512,256]{2,1,0:T(8,128)(2,1)S(1)}, u32[]{:S(2)}, u32[]{:S(2)}) collective-permute-start(bf16[2,512,256]{2,1,0:T(8,128)(2,1)S(1)} %get-tuple-element.16), channel_id=1, source_target_pairs={{0,8},{1,17},{2,10},{3,19},{4,12},{5,21},{6,14},{7,23},{8,0},{9,25... | collective-permute-start | bytes 1572872 | tf_op jit(solution)/shard_map/ppermute | solution.py:213
  92.6 15.9 %collective-permute-start.12 = (bf16[2,512,256]{2,1,0:T(8,128)(2,1)S(1)}, bf16[2,512,256]{2,1,0:T(8,128)(2,1)S(1)}, u32[]{:S(2)}, u32[]{:S(2)}) collective-permute-start(bf16[2,512,256]{2,1,0:T(8,128)(2,1)S(1)} %get-tuple-element.14), channel_id=1, source_target_pairs={{0,8},{1,17},{2,10},{3,19},{4,12},{5,21},{6,14},{7,23},{8,0},{9,25... | collective-permute-start | bytes 1572872 | tf_op jit(solution)/shard_map/ppermute | solution.py:213
  97.5 12.2 %collective-permute-start.21 = (bf16[512,256]{1,0:T(8,128)(2,1)S(1)}, bf16[512,256]{1,0:T(8,128)(2,1)S(1)}, u32[]{:S(2)}, u32[]{:S(2)}) collective-permute-start(bf16[512,256]{1,0:T(8,128)(2,1)S(1)} %fusion.3), channel_id=1, source_target_pairs={{0,16},{1,9},{2,18},{3,11},{4,20},{5,13},{6,22},{7,15},{8,24},{9,1... | collective-permute-start | bytes 786440 | tf_op jit(solution)/shard_map/ppermute | solution.py:213
  108.5 5.3 %collective-permute-start.13 = (bf16[512,256]{1,0:T(8,128)(2,1)S(1)}, bf16[512,256]{1,0:T(8,128)(2,1)S(1)}, u32[]{:S(2)}, u32[]{:S(2)}) collective-permute-start(bf16[512,256]{1,0:T(8,128)(2,1)S(1)} %fusion.2), channel_id=1, source_target_pairs={{0,16},{1,9},{2,18},{3,11},{4,20},{5,13},{6,22},{7,15},{8,24},{9,1... | collective-permute-start | bytes 786440 | tf_op jit(solution)/shard_map/ppermute | solution.py:213
  (1 other events, 5.0 us)

commit v3 on v2

v3 whole, which is shorter than its diff:
```python
import functools
import jax
import jax.numpy as jnp
from jax import lax
from jax.experimental import pallas as pl
from jax.experimental.pallas import tpu as pltpu
from jax.sharding import PartitionSpec as P

HD = 128
BLOCK = 128
MOSTB = 16
STEP = 4
TOGETHER = 4
MASKED = -1e30
EXP2_SCALE = HD ** (-0.5) * 1.4426950408889634
VMEM = pl.BlockSpec(memory_space=pltpu.VMEM)
SMEM = pl.BlockSpec(memory_space=pltpu.SMEM)
ANY = pl.BlockSpec(memory_space=pl.ANY)


def gather_rows(own, other, near, near_other, far, far_other, keys, values):
    tokens = own.shape[1]
    odd = lax.rem(lax.axis_index("docs"), 2)

    def place(index, piece):
        start = pl.multiple_of(index * tokens, BLOCK)
        keys[pl.ds(start, tokens), :] = piece[0]
        values[pl.ds(start, tokens), :HD] = piece[1]

    values[:, HD:] = jnp.ones((values.shape[0], HD), values.dtype)
    place(0 + odd, far)
    place(1 - odd, far_other)
    place(2 + odd, near)
    place(3 - odd, near_other)
    place(4 + odd, own)
    place(5 - odd, other)


def prepare(pieces):
    rows = len(pieces) * pieces[0].shape[1]
    return pl.pallas_call(
        gather_rows,
        out_shape=(
            jax.ShapeDtypeStruct((rows, HD), jnp.bfloat16),
            jax.ShapeDtypeStruct((rows, 2 * HD), jnp.bfloat16),
        ),
        in_specs=[VMEM] * len(pieces),
        out_specs=(VMEM, VMEM),
        compiler_params=pltpu.CompilerParams(vmem_limit_bytes=12 << 20),
        name="prepare",
    )(*pieces)


def attend(docs, query, keys, values, *refs, first, heads_together):
    out, scores = refs[-2:]
    heads = query.shape[1] // HD
    rows = heads_together * BLOCK
    shard = lax.axis_index("docs")
    local_blocks = keys.shape[0] // 6 // BLOCK
    place_in = shard * local_blocks + first
    begin = jnp.int32(0)
    edge = jnp.int32(0)
    for doc in range(docs.shape[0]):
        edge = edge + docs[doc]
        begin = jnp.where(edge <= place_in, edge, begin)
    count = place_in - begin + 1
    last = (4 + lax.rem(shard, 2)) * local_blocks + first
    start = pl.multiple_of((last - (MOSTB - 1)) * BLOCK, BLOCK)
    span = STEP * BLOCK
    bias = [jnp.where(MOSTB - 1 - block < count, 0.0, MASKED) for block in range(MOSTB)]
    down = lax.broadcasted_iota(jnp.int32, (rows, BLOCK), 0) % BLOCK
    across = lax.broadcasted_iota(jnp.int32, (rows, BLOCK), 1)
    causal = across <= down

    def score(team):
        slot = team % 2
        left = jnp.concatenate(
            [query[:, h * HD : (h + 1) * HD] for h in range(team * heads_together, (team + 1) * heads_together)]
        )
        high = None
        for chunk in range(MOSTB // STEP):
            got = lax.dot_general(
                left, keys[pl.ds(start + chunk * span, span), :], (((1,), (1,)), ((), ())),
                preferred_element_type=jnp.float32,
            )
            for block in range(STEP):
                number = chunk * STEP + block
                piece = got[:, block * BLOCK : (block + 1) * BLOCK]
                if number == MOSTB - 1:
                    piece = jnp.where(causal, piece, MASKED)
                else:
                    piece = piece + bias[number]
                scores[slot, :, number * BLOCK : (number + 1) * BLOCK] = piece
                high = piece if high is None else jnp.maximum(high, piece)
        return jnp.max(high, axis=1, keepdims=True)

    def weigh(team, top):
        slot = team % 2
        top = jnp.broadcast_to(top, (rows, BLOCK))
        total = None
        for chunk in range(MOSTB // STEP):
            here = slice(chunk * span, (chunk + 1) * span)
            raised = jnp.exp2((scores[slot, :, here] - jnp.concatenate([top] * STEP, axis=1)) * EXP2_SCALE)
            part = jnp.dot(
                raised.astype(jnp.bfloat16), values[pl.ds(start + chunk * span, span), :],
                preferred_element_type=jnp.float32,
            )
            total = part if total is None else total + part
        done = (total[:, :HD] / total[:, HD:]).astype(out.dtype)
        for j in range(heads_together):
            h = team * heads_together + j
            out[:, h * HD : (h + 1) * HD] = done[j * BLOCK : (j + 1) * BLOCK, :]

    teams = heads // heads_together
    top = score(0)
    for team in range(teams):
        following = score(team + 1) if team + 1 < teams else None
        weigh(team, top)
        top = following


def attention(docs, query, keys, values, part, before):
    tokens, width = query.shape
    together = TOGETHER
    return pl.pallas_call(
        functools.partial(attend, first=part, heads_together=together),
        out_shape=jax.ShapeDtypeStruct((tokens, width), jnp.bfloat16),
        grid=(1,),
        in_specs=[SMEM, pl.BlockSpec((BLOCK, width), lambda i: (part, 0)), VMEM, VMEM] + [ANY] * len(before),
        out_specs=pl.BlockSpec((BLOCK, width), lambda i: (part, 0)),
        input_output_aliases={4: 0} if before else {},
        scratch_shapes=[
            pltpu.VMEM((2, together * BLOCK, MOSTB * BLOCK), jnp.float32),
        ],
        compiler_params=pltpu.CompilerParams(vmem_limit_bytes=24 << 20),
        name="attend",
    )(docs, query, keys, values, *before)


def project(attended, pieces, half, first_slot, slots):
    tokens, depth = attended.shape
    width = pieces[0].shape[1]

    def body(left, *refs):
        sources = refs[: len(pieces)]
        out, rights, sems = refs[len(pieces) :]
        shard = lax.axis_index("docs")
        group = lax.axis_index("heads")
        odd = lax.rem(shard, 2)
        plane = lax.div(shard, 2)
        early = jnp.where(odd == 1, 2, 1)
        late = 3 - early
        targets = [group ^ early, group ^ 3, group, group ^ late]
        for slot, target in enumerate(targets[first_slot : first_slot + slots]):
            distance = jnp.abs(plane - target)
            below = jnp.where(target < plane, 1, 0)
            away = 2 * distance + (below ^ odd)
            index = jnp.where(distance == 0, odd ^ half, away)
            for j, source in enumerate(sources):
                @pl.when(index == j)
                def _(source=source, slot=slot):
                    pltpu.make_async_copy(source, rights.at[slot], sems.at[slot]).start()
        for slot in range(slots):
            pltpu.make_async_copy(sources[0], rights.at[slot], sems.at[slot]).wait()
            out[slot] = jnp.dot(
                left[...], rights[slot], preferred_element_type=jnp.float32
            ).astype(jnp.bfloat16)

    shape = jax.ShapeDtypeStruct((slots, tokens, width), jnp.bfloat16)
    return pl.pallas_call(
        body,
        out_shape=shape,
        in_specs=[VMEM] + [ANY] * len(pieces),
        out_specs=VMEM,
        scratch_shapes=[pltpu.VMEM((slots, depth, width), jnp.bfloat16), pltpu.SemaphoreType.DMA((slots,))],
        compiler_params=pltpu.CompilerParams(vmem_limit_bytes=16 << 20),
        name="project",
    )(attended, *pieces)


def build(shards, groups):
    def send(block, route, axis="docs"):
        return lax.ppermute(block, axis, route)

    planes = shards // 2
    swap = [(i, i ^ 1) for i in range(shards)]

    def up(step):
        return [(i, i + 2) for i in range(2 * (step - 1), shards - 2)]

    def cross(step):
        route = []
        for p in range(planes - 1):
            if p >= step - 1:
                route.append((2 * p + (step > 1), 2 * p + 3))
            if p + 1 <= planes - step:
                route.append((2 * p + 2 + (step == 1), 2 * p))
        return route

    def exchange(block, early):
        route = []
        for group in range(groups):
            for shard in range(shards):
                flip = 1 if (shard % 2 == 0) == early else 2
                route.append((group * shards + shard, (group ^ flip) * shards + shard))
        return send(block, route, ("heads", "docs"))

    def local(query_rows, key_rows, value_rows, doc_blocks, out_weight):
        return inside(query_rows, key_rows, value_rows, doc_blocks, out_weight)

    def inside(query_rows, key_rows, value_rows, doc_blocks, out_weight):
        f32 = jnp.float32
        own = jnp.stack([key_rows, value_rows])
        other = send(own, swap)
        near = send(own, up(1))
        near_other = send(near, swap)
        far = send(near, up(2))
        far_other = send(far, swap)
        keys, values = prepare((own, other, near, near_other, far, far_other))
        before = ()
        for part in range(own.shape[1] // BLOCK):
            attended = attention(doc_blocks, query_rows, keys, values, part, before)
            before = (attended,)

        if shards != 2 * groups:
            weight = lax.all_gather(out_weight, "docs", axis=1, tiled=True)
            partial = jnp.dot(attended, weight, preferred_element_type=f32)
            return lax.psum_scatter(
                partial.astype(jnp.bfloat16), "heads", scatter_dimension=1, tiled=True
            )

        weight_other = send(out_weight, swap)
        pieces = []
        for last in (out_weight, weight_other):
            found = [out_weight, weight_other]
            for step in range(1, shards // 2):
                last = send(last, cross(step))
                found += [last, send(last, swap)]
            pieces.append(found)
        results = []
        for half in range(2):
            outward = project(attended, pieces[half], half, 0, 2)
            arrived = exchange(outward, True)
            keep = project(attended, pieces[half], half, 2, 2)
            onward = (keep[1].astype(f32) + arrived[1].astype(f32)).astype(jnp.bfloat16)
            final = exchange(onward, False)
            results.append((keep[0].astype(f32) + arrived[0].astype(f32) + final.astype(f32)).astype(jnp.bfloat16))
        ahead = lax.axis_index("heads") > lax.axis_index("docs") // 2
        return jnp.concatenate(
            [jnp.where(ahead, results[1], results[0]), jnp.where(ahead, results[0], results[1])], axis=1
        )

    return local


def solution(mesh):
    placed = (P("docs", "heads"), P("docs", "heads"), P("docs", "heads"), P(), P("heads", "docs"))
    shards, groups = mesh.shape["docs"], mesh.shape["heads"]
    return jax.shard_map(
        build(shards, groups), mesh=mesh, in_specs=placed, out_specs=P("docs", "heads"), check_vma=False
    )
```

time: 115 us -> 91.9 us (0.80)
  the two profiles are of different devices: /device:TPU:9 before, /device:TPU:16 now
where the time goes in v3:
time: 91.9 us; the launch traced here: 91 us
  starting transfers between devices  34.5 us (38%)
  waiting for transfers between devices  33.7 us (37%)
  Pallas kernels  20.4 us (22%)
  other arithmetic  2.18 us (2%)
    ppermute x22, starting transfers between devices, send(): return lax.ppermute(block, axis, route)  34.5 us
    ppermute x22, waiting for transfers between devices, send(): return lax.ppermute(block, axis, route)  33.7 us
    pallas_call x4, Pallas kernels, attention(): pl.pallas_call(functools.partial(attend, first=part, heads_together=toget...  13.9 us
    pallas_call x4, Pallas kernels, project(): pl.pallas_call(body, out_shape=shape, in_specs=[VMEM] + [ANY] * len(piece...  6.21 us
  transfers between devices with their start and end apart: 22, of which 8 were waited for; matrix products, arithmetic and copies ran while one was open for 1% of the time, Pallas kernels for 22%

profile of v3, /device:TPU:16, one launch (start us, length us, event | category | flops | bytes accessed | tf_op | source)
XLA Modules:
  0.0 91.0 jit_solution(18398328887817571013)
XLA Ops:
  0.0 3.6 %collective-permute-start.14 = (bf16[1024,256]{1,0:T(8,128)(2,1)}, bf16[1024,256]{1,0:T(8,128)(2,1)S(1)}, u32[]{:S(2)}, u32[]{:S(2)}) collective-permute-start(bf16[1024,256]{1,0:T(8,128)(2,1)} %refs_0_.7), channel_id=1, source_target_pairs={{0,3},{3,0},{2,5},{5,2},{4,7},{7,4},{8,11},{11,8},{10,13},{13,10},... | collective-permute-start | bytes 1572872 | tf_op jit(solution)/shard_map/ppermute | solution.py:183
  3.6 2.1 %collective-permute-start.6 = (bf16[1024,256]{1,0:T(8,128)(2,1)S(1)}, bf16[1024,256]{1,0:T(8,128)(2,1)S(1)}, u32[]{:S(2)}, u32[]{:S(2)}) collective-permute-start(bf16[1024,256]{1,0:T(8,128)(2,1)S(1)} %collective-permute-done.5.refs_1_), channel_id=1, source_target_pairs={{0,3},{3,0},{2,5},{5,2},{4,7},{7,4},{8,11},{11,8},{10,13},{13,10},... | collective-permute-start | bytes 1572872 | tf_op jit(solution)/shard_map/ppermute | solution.py:183
  5.7 5.1 %collective-permute-done.14.refs_2_ = bf16[1024,256]{1,0:T(8,128)(2,1)S(1)} collective-permute-done((bf16[1024,256]{1,0:T(8,128)(2,1)}, bf16[1024,256]{1,0:T(8,128)(2,1)S(1)}, u32[]{:S(2)}, u32[]{:S(2)}) %collective-permute-start.14) | collective-permute-done | bytes 524320 | tf_op jit(solution)/shard_map/ppermute | solution.py:183
  10.9 2.4 %collective-permute-start.16 = (bf16[1024,256]{1,0:T(8,128)(2,1)S(1)}, bf16[1024,256]{1,0:T(8,128)(2,1)S(1)}, u32[]{:S(2)}, u32[]{:S(2)}) collective-permute-start(bf16[1024,256]{1,0:T(8,128)(2,1)S(1)} %collective-permute-done.14.refs_2_), channel_id=1, source_target_pairs={{2,0},{3,5},{4,2},{5,7},{10,8},{11,13},{12,10},{13,15},{18,16},{19... | collective-permute-start | bytes 1572872 | tf_op jit(solution)/shard_map/ppermute | solution.py:183
  13.2 4.2 %collective-permute-done.6.refs_2_ = bf16[1024,256]{1,0:T(8,128)(2,1)S(1)} collective-permute-done((bf16[1024,256]{1,0:T(8,128)(2,1)S(1)}, bf16[1024,256]{1,0:T(8,128)(2,1)S(1)}, u32[]{:S(2)}, u32[]{:S(2)}) %collective-permute-start.6) | collective-permute-done | bytes 524320 | tf_op jit(solution)/shard_map/ppermute | solution.py:183
  17.4 2.1 %collective-permute-start.8 = (bf16[1024,256]{1,0:T(8,128)(2,1)S(1)}, bf16[1024,256]{1,0:T(8,128)(2,1)S(1)}, u32[]{:S(2)}, u32[]{:S(2)}) collective-permute-start(bf16[1024,256]{1,0:T(8,128)(2,1)S(1)} %collective-permute-done.6.refs_2_), channel_id=1, source_target_pairs={{2,0},{3,5},{4,2},{5,7},{10,8},{11,13},{12,10},{13,15},{18,16},{19... | collective-permute-start | bytes 1572872 | tf_op jit(solution)/shard_map/ppermute | solution.py:183
  20.5 1.9 %collective-permute-start.1 = (bf16[2,512,128]{2,1,0:T(8,128)(2,1)S(1)}, bf16[2,512,128]{2,1,0:T(8,128)(2,1)S(1)}, u32[]{:S(2)}, u32[]{:S(2)}) collective-permute-start(bf16[2,512,128]{2,1,0:T(8,128)(2,1)S(1)} %pad_maximum_fusion.1.own), channel_id=1, source_target_pairs={{0,2},{1,3},{2,4},{3,5},{4,6},{5,7},{8,10},{9,11},{10,12},{11,13},... | collective-permute-start | bytes 786440 | tf_op jit(solution)/shard_map/ppermute | solution.py:183
  22.4 1.9 %collective-permute-start = (bf16[2,512,128]{2,1,0:T(8,128)(2,1)S(1)}, bf16[2,512,128]{2,1,0:T(8,128)(2,1)S(1)}, u32[]{:S(2)}, u32[]{:S(2)}) collective-permute-start(bf16[2,512,128]{2,1,0:T(8,128)(2,1)S(1)} %pad_maximum_fusion.1.own), channel_id=1, source_target_pairs={{0,1},{1,0},{2,3},{3,2},{4,5},{5,4},{6,7},{7,6},{8,9},{9,8},{10,11... | collective-permute-start | bytes 786440 | tf_op jit(solution)/shard_map/ppermute | solution.py:183
  25.0 6.5 %collective-permute-done.1.near = bf16[2,512,128]{2,1,0:T(8,128)(2,1)S(1)} collective-permute-done((bf16[2,512,128]{2,1,0:T(8,128)(2,1)S(1)}, bf16[2,512,128]{2,1,0:T(8,128)(2,1)S(1)}, u32[]{:S(2)}, u32[]{:S(2)}) %collective-permute-start.1) | collective-permute-done | bytes 262176 | tf_op jit(solution)/shard_map/ppermute | solution.py:183
  31.6 1.9 %collective-permute-start.3 = (bf16[2,512,128]{2,1,0:T(8,128)(2,1)S(1)}, bf16[2,512,128]{2,1,0:T(8,128)(2,1)S(1)}, u32[]{:S(2)}, u32[]{:S(2)}) collective-permute-start(bf16[2,512,128]{2,1,0:T(8,128)(2,1)S(1)} %collective-permute-done.1.near), channel_id=1, source_target_pairs={{2,4},{3,5},{4,6},{5,7},{10,12},{11,13},{12,14},{13,15},{18,20},{1... | collective-permute-start | bytes 786440 | tf_op jit(solution)/shard_map/ppermute | solution.py:183
  33.5 3.5 %collective-permute-start.15 = (bf16[1024,256]{1,0:T(8,128)(2,1)S(1)}, bf16[1024,256]{1,0:T(8,128)(2,1)S(1)}, u32[]{:S(2)}, u32[]{:S(2)}) collective-permute-start(bf16[1024,256]{1,0:T(8,128)(2,1)S(1)} %collective-permute-done.14.refs_2_), channel_id=1, source_target_pairs={{0,1},{1,0},{2,3},{3,2},{4,5},{5,4},{6,7},{7,6},{8,9},{9,8},{10,11... | collective-permute-start | bytes 1572872 | tf_op jit(solution)/shard_map/ppermute | solution.py:183
  38.4 3.1 %collective-permute-done.3.far = bf16[2,512,128]{2,1,0:T(8,128)(2,1)S(1)} collective-permute-done((bf16[2,512,128]{2,1,0:T(8,128)(2,1)S(1)}, bf16[2,512,128]{2,1,0:T(8,128)(2,1)S(1)}, u32[]{:S(2)}, u32[]{:S(2)}) %collective-permute-start.3) | collective-permute-done | bytes 262176 | tf_op jit(solution)/shard_map/ppermute | solution.py:183
  41.5 2.8 %collective-permute-start.4 = (bf16[2,512,128]{2,1,0:T(8,128)(2,1)S(1)}, bf16[2,512,128]{2,1,0:T(8,128)(2,1)S(1)}, u32[]{:S(2)}, u32[]{:S(2)}) collective-permute-start(bf16[2,512,128]{2,1,0:T(8,128)(2,1)S(1)} %collective-permute-done.3.far), channel_id=1, source_target_pairs={{0,1},{1,0},{2,3},{3,2},{4,5},{5,4},{6,7},{7,6},{8,9},{9,8},{10,11... | collective-permute-start | bytes 786440 | tf_op jit(solution)/shard_map/ppermute | solution.py:183
  46.0 3.9 %collective-permute-start.11 = (bf16[1024,256]{1,0:T(8,128)(2,1)S(1)}, bf16[1024,256]{1,0:T(8,128)(2,1)S(1)}, u32[]{:S(2)}, u32[]{:S(2)}) collective-permute-start(bf16[1024,256]{1,0:T(8,128)(2,1)S(1)} %collective-permute-done.10.refs_6_), channel_id=1, source_target_pairs={{0,1},{1,0},{2,3},{3,2},{4,5},{5,4},{6,7},{7,6},{8,9},{9,8},{10,11... | collective-permute-start | bytes 1572872 | tf_op jit(solution)/shard_map/ppermute | solution.py:183
  50.2 3.4 %attend.4.refs_0_ = bf16[512,1024]{1,0:T(8,128)(2,1)S(1)} custom-call(s32[4]{0:T(128)S(1)} %copy-done.2, bf16[512,1024]{1,0:T(8,128)(2,1)S(1)} %copy-done, bf16[3072,128]{1,0:T(8,128)(2,1)S(1)} %get-tuple-element.7.keys, bf16[3072,256]{1,0:T(8,128)(2,1)S(1)} %get-tuple-element.8.values), custom_call_target="tpu_custom_call" | custom-call | tf_op jit(solution)/shard_map/attend/pallas_call | solution.py:125
  53.7 3.4 %attend.5.refs_0_ = bf16[512,1024]{1,0:T(8,128)(2,1)S(1)} custom-call(s32[4]{0:T(128)S(1)} %copy-done.2, bf16[512,1024]{1,0:T(8,128)(2,1)S(1)} %copy-done, bf16[3072,128]{1,0:T(8,128)(2,1)S(1)} %get-tuple-element.7.keys, bf16[3072,256]{1,0:T(8,128)(2,1)S(1)} %get-tuple-element.8.values, ...), custom_call_target="tpu_custom_call", output_to_operand_aliasing={{}: (4, {})} | custom-call | tf_op jit(solution)/shard_map/attend/pallas_call | solution.py:125
  57.1 3.4 %attend.6.refs_0_ = bf16[512,1024]{1,0:T(8,128)(2,1)S(1)} custom-call(s32[4]{0:T(128)S(1)} %copy-done.2, bf16[512,1024]{1,0:T(8,128)(2,1)S(1)} %copy-done, bf16[3072,128]{1,0:T(8,128)(2,1)S(1)} %get-tuple-element.7.keys, bf16[3072,256]{1,0:T(8,128)(2,1)S(1)} %get-tuple-element.8.values, ...), custom_call_target="tpu_custom_call", output_to_operand_aliasing={{}: (4, {})} | custom-call | tf_op jit(solution)/shard_map/attend/pallas_call | solution.py:125
  60.5 3.6 %attend.7.left = bf16[512,1024]{1,0:T(8,128)(2,1)S(1)} custom-call(s32[4]{0:T(128)S(1)} %copy-done.2, bf16[512,1024]{1,0:T(8,128)(2,1)S(1)} %copy-done, bf16[3072,128]{1,0:T(8,128)(2,1)S(1)} %get-tuple-element.7.keys, bf16[3072,256]{1,0:T(8,128)(2,1)S(1)} %get-tuple-element.8.values, bf16[512,1024]{1,0:T(8,128)(2,1)S(1)} %attend.6.refs_0_), custom_call_target="tpu_custom_call", output_to_operand_aliasing={{}: (4, {})} | custom-call | tf_op jit(solution)/shard_map/attend/pallas_call | solution.py:125
  67.4 1.6 %project.5 = bf16[2,512,256]{2,1,0:T(8,128)(2,1)S(1)} custom-call(bf16[512,1024]{1,0:T(8,128)(2,1)S(1)} %attend.7.left, bf16[1024,256]{1,0:T(8,128)(2,1)S(1)} %copy-done.1, bf16[1024,256]{1,0:T(8,128)(2,1)S(1)} %collective-permute-done.5.refs_1_, bf16[1024,256]{1,0:T(8,128)(2,1)S(1)} %collective-permute-done.6.refs_2_, ...), custom_call_target="tpu_custom_call" | custom-call | tf_op jit(solution)/shard_map/project/pallas_call | solution.py:170
  71.1 4.0 %collective-permute-done.20 = bf16[2,512,256]{2,1,0:T(8,128)(2,1)S(1)} collective-permute-done((bf16[2,512,256]{2,1,0:T(8,128)(2,1)S(1)}, bf16[2,512,256]{2,1,0:T(8,128)(2,1)S(1)}, u32[]{:S(2)}, u32[]{:S(2)}) %collective-permute-start.20) | collective-permute-done | bytes 524320 | tf_op jit(solution)/shard_map/ppermute | solution.py:183
  75.1 1.6 %collective-permute-start.21 = (bf16[512,256]{1,0:T(8,128)(2,1)S(1)}, bf16[512,256]{1,0:T(8,128)(2,1)S(1)}, u32[]{:S(2)}, u32[]{:S(2)}) collective-permute-start(bf16[512,256]{1,0:T(8,128)(2,1)S(1)} %fusion.3), channel_id=1, source_target_pairs={{0,16},{1,9},{2,18},{3,11},{4,20},{5,13},{6,22},{7,15},{8,24},{9,1... | collective-permute-start | bytes 786440 | tf_op jit(solution)/shard_map/ppermute | solution.py:183
  78.2 5.2 %collective-permute-done.12 = bf16[2,512,256]{2,1,0:T(8,128)(2,1)S(1)} collective-permute-done((bf16[2,512,256]{2,1,0:T(8,128)(2,1)S(1)}, bf16[2,512,256]{2,1,0:T(8,128)(2,1)S(1)}, u32[]{:S(2)}, u32[]{:S(2)}) %collective-permute-start.12) | collective-permute-done | bytes 524320 | tf_op jit(solution)/shard_map/ppermute | solution.py:183
  83.5 1.6 %collective-permute-start.13 = (bf16[512,256]{1,0:T(8,128)(2,1)S(1)}, bf16[512,256]{1,0:T(8,128)(2,1)S(1)}, u32[]{:S(2)}, u32[]{:S(2)}) collective-permute-start(bf16[512,256]{1,0:T(8,128)(2,1)S(1)} %fusion.2), channel_id=1, source_target_pairs={{0,16},{1,9},{2,18},{3,11},{4,20},{5,13},{6,22},{7,15},{8,24},{9,1... | collective-permute-start | bytes 786440 | tf_op jit(solution)/shard_map/ppermute | solution.py:183
  85.1 4.8 %collective-permute-done.13 = bf16[512,256]{1,0:T(8,128)(2,1)S(1)} collective-permute-done((bf16[512,256]{1,0:T(8,128)(2,1)S(1)}, bf16[512,256]{1,0:T(8,128)(2,1)S(1)}, u32[]{:S(2)}, u32[]{:S(2)}) %collective-permute-start.13) | collective-permute-done | bytes 262176 | tf_op jit(solution)/shard_map/ppermute | solution.py:183
  (40 shorter events, 13.0 us)
Async XLA Ops:
  0.0 50.2 %copy-start = (bf16[512,1024]{1,0:T(8,128)(2,1)S(1)}, bf16[512,1024]{1,0:T(8,128)(2,1)}, u32[]{:S(2)}) copy-start(bf16[512,1024]{1,0:T(8,128)(2,1)} %query.7) | copy-start | bytes 3145732
  0.0 50.2 %copy-start.2 = (s32[4]{0:T(128)S(1)}, s32[4]{0:T(128)}, u32[]{:S(2)}) copy-start(s32[4]{0:T(128)} %docs.7) | copy-start | bytes 52
  0.0 3.6 %collective-permute-start.5 = (bf16[1024,256]{1,0:T(8,128)(2,1)}, bf16[1024,256]{1,0:T(8,128)(2,1)S(1)}, u32[]{:S(2)}, u32[]{:S(2)}) collective-permute-start(bf16[1024,256]{1,0:T(8,128)(2,1)} %refs_0_.7), channel_id=1, source_target_pairs={{0,1},{1,0},{2,3},{3,2},{4,5},{5,4},{6,7},{7,6},{8,9},{9,8},{10,11... | collective-permute-start | bytes 1572872 | tf_op jit(solution)/shard_map/ppermute | solution.py:183
  0.0 10.8 %collective-permute-start.14 = (bf16[1024,256]{1,0:T(8,128)(2,1)}, bf16[1024,256]{1,0:T(8,128)(2,1)S(1)}, u32[]{:S(2)}, u32[]{:S(2)}) collective-permute-start(bf16[1024,256]{1,0:T(8,128)(2,1)} %refs_0_.7), channel_id=1, source_target_pairs={{0,3},{3,0},{2,5},{5,2},{4,7},{7,4},{8,11},{11,8},{10,13},{13,10},... | collective-permute-start | bytes 1572872 | tf_op jit(solution)/shard_map/ppermute | solution.py:183
  3.6 13.8 %collective-permute-start.6 = (bf16[1024,256]{1,0:T(8,128)(2,1)S(1)}, bf16[1024,256]{1,0:T(8,128)(2,1)S(1)}, u32[]{:S(2)}, u32[]{:S(2)}) collective-permute-start(bf16[1024,256]{1,0:T(8,128)(2,1)S(1)} %collective-permute-done.5.refs_1_), channel_id=1, source_target_pairs={{0,3},{3,0},{2,5},{5,2},{4,7},{7,4},{8,11},{11,8},{10,13},{13,10},... | collective-permute-start | bytes 1572872 | tf_op jit(solution)/shard_map/ppermute | solution.py:183
  10.9 13.5 %collective-permute-start.16 = (bf16[1024,256]{1,0:T(8,128)(2,1)S(1)}, bf16[1024,256]{1,0:T(8,128)(2,1)S(1)}, u32[]{:S(2)}, u32[]{:S(2)}) collective-permute-start(bf16[1024,256]{1,0:T(8,128)(2,1)S(1)} %collective-permute-done.14.refs_2_), channel_id=1, source_target_pairs={{2,0},{3,5},{4,2},{5,7},{10,8},{11,13},{12,10},{13,15},{18,16},{19... | collective-permute-start | bytes 1572872 | tf_op jit(solution)/shard_map/ppermute | solution.py:183
  17.4 19.5 %collective-permute-start.8 = (bf16[1024,256]{1,0:T(8,128)(2,1)S(1)}, bf16[1024,256]{1,0:T(8,128)(2,1)S(1)}, u32[]{:S(2)}, u32[]{:S(2)}) collective-permute-start(bf16[1024,256]{1,0:T(8,128)(2,1)S(1)} %collective-permute-done.6.refs_2_), channel_id=1, source_target_pairs={{2,0},{3,5},{4,2},{5,7},{10,8},{11,13},{12,10},{13,15},{18,16},{19... | collective-permute-start | bytes 1572872 | tf_op jit(solution)/shard_map/ppermute | solution.py:183
  20.5 11.1 %collective-permute-start.1 = (bf16[2,512,128]{2,1,0:T(8,128)(2,1)S(1)}, bf16[2,512,128]{2,1,0:T(8,128)(2,1)S(1)}, u32[]{:S(2)}, u32[]{:S(2)}) collective-permute-start(bf16[2,512,128]{2,1,0:T(8,128)(2,1)S(1)} %pad_maximum_fusion.1.own), channel_id=1, source_target_pairs={{0,2},{1,3},{2,4},{3,5},{4,6},{5,7},{8,10},{9,11},{10,12},{11,13},... | collective-permute-start | bytes 786440 | tf_op jit(solution)/shard_map/ppermute | solution.py:183
  22.4 15.2 %collective-permute-start = (bf16[2,512,128]{2,1,0:T(8,128)(2,1)S(1)}, bf16[2,512,128]{2,1,0:T(8,128)(2,1)S(1)}, u32[]{:S(2)}, u32[]{:S(2)}) collective-permute-start(bf16[2,512,128]{2,1,0:T(8,128)(2,1)S(1)} %pad_maximum_fusion.1.own), channel_id=1, source_target_pairs={{0,1},{1,0},{2,3},{3,2},{4,5},{5,4},{6,7},{7,6},{8,9},{9,8},{10,11... | collective-permute-start | bytes 786440 | tf_op jit(solution)/shard_map/ppermute | solution.py:183
  24.3 20.0 %collective-permute-start.18 = (bf16[1024,256]{1,0:T(8,128)(2,1)S(1)}, bf16[1024,256]{1,0:T(8,128)(2,1)S(1)}, u32[]{:S(2)}, u32[]{:S(2)}) collective-permute-start(bf16[1024,256]{1,0:T(8,128)(2,1)S(1)} %collective-permute-done.16.refs_4_), channel_id=1, source_target_pairs={{2,0},{5,7},{10,8},{13,15},{18,16},{21,23},{26,24},{29,31}} | collective-permute-start | bytes 1572872 | tf_op jit(solution)/shard_map/ppermute | solution.py:183
  31.6 9.9 %collective-permute-start.3 = (bf16[2,512,128]{2,1,0:T(8,128)(2,1)S(1)}, bf16[2,512,128]{2,1,0:T(8,128)(2,1)S(1)}, u32[]{:S(2)}, u32[]{:S(2)}) collective-permute-start(bf16[2,512,128]{2,1,0:T(8,128)(2,1)S(1)} %collective-permute-done.1.near), channel_id=1, source_target_pairs={{2,4},{3,5},{4,6},{5,7},{10,12},{11,13},{12,14},{13,15},{18,20},{1... | collective-permute-start | bytes 786440 | tf_op jit(solution)/shard_map/ppermute | solution.py:183
  33.5 12.4 %collective-permute-start.15 = (bf16[1024,256]{1,0:T(8,128)(2,1)S(1)}, bf16[1024,256]{1,0:T(8,128)(2,1)S(1)}, u32[]{:S(2)}, u32[]{:S(2)}) collective-permute-start(bf16[1024,256]{1,0:T(8,128)(2,1)S(1)} %collective-permute-done.14.refs_2_), channel_id=1, source_target_pairs={{0,1},{1,0},{2,3},{3,2},{4,5},{5,4},{6,7},{7,6},{8,9},{9,8},{10,11... | collective-permute-start | bytes 1572872 | tf_op jit(solution)/shard_map/ppermute | solution.py:183
  37.0 9.0 %collective-permute-start.10 = (bf16[1024,256]{1,0:T(8,128)(2,1)S(1)}, bf16[1024,256]{1,0:T(8,128)(2,1)S(1)}, u32[]{:S(2)}, u32[]{:S(2)}) collective-permute-start(bf16[1024,256]{1,0:T(8,128)(2,1)S(1)} %collective-permute-done.8.refs_4_), channel_id=1, source_target_pairs={{2,0},{5,7},{10,8},{13,15},{18,16},{21,23},{26,24},{29,31}} | collective-permute-start | bytes 1572872 | tf_op jit(solution)/shard_map/ppermute | solution.py:183
  37.7 6.7 %collective-permute-start.2 = (bf16[2,512,128]{2,1,0:T(8,128)(2,1)S(1)}, bf16[2,512,128]{2,1,0:T(8,128)(2,1)S(1)}, u32[]{:S(2)}, u32[]{:S(2)}) collective-permute-start(bf16[2,512,128]{2,1,0:T(8,128)(2,1)S(1)} %collective-permute-done.1.near), channel_id=1, source_target_pairs={{0,1},{1,0},{2,3},{3,2},{4,5},{5,4},{6,7},{7,6},{8,9},{9,8},{10,11... | collective-permute-start | bytes 786440 | tf_op jit(solution)/shard_map/ppermute | solution.py:183
  41.5 4.0 %collective-permute-start.4 = (bf16[2,512,128]{2,1,0:T(8,128)(2,1)S(1)}, bf16[2,512,128]{2,1,0:T(8,128)(2,1)S(1)}, u32[]{:S(2)}, u32[]{:S(2)}) collective-permute-start(bf16[2,512,128]{2,1,0:T(8,128)(2,1)S(1)} %collective-permute-done.3.far), channel_id=1, source_target_pairs={{0,1},{1,0},{2,3},{3,2},{4,5},{5,4},{6,7},{7,6},{8,9},{9,8},{10,11... | collective-permute-start | bytes 786440 | tf_op jit(solution)/shard_map/ppermute | solution.py:183
  44.3 19.9 %collective-permute-start.17 = (bf16[1024,256]{1,0:T(8,128)(2,1)S(1)}, bf16[1024,256]{1,0:T(8,128)(2,1)S(1)}, u32[]{:S(2)}, u32[]{:S(2)}) collective-permute-start(bf16[1024,256]{1,0:T(8,128)(2,1)S(1)} %collective-permute-done.16.refs_4_), channel_id=1, source_target_pairs={{0,1},{1,0},{2,3},{3,2},{4,5},{5,4},{6,7},{7,6},{8,9},{9,8},{10,11... | collective-permute-start | bytes 1572872 | tf_op jit(solution)/shard_map/ppermute | solution.py:183
  44.3 19.9 %collective-permute-start.19 = (bf16[1024,256]{1,0:T(8,128)(2,1)S(1)}, bf16[1024,256]{1,0:T(8,128)(2,1)S(1)}, u32[]{:S(2)}, u32[]{:S(2)}) collective-permute-start(bf16[1024,256]{1,0:T(8,128)(2,1)S(1)} %collective-permute-done.18.refs_6_), channel_id=1, source_target_pairs={{0,1},{1,0},{2,3},{3,2},{4,5},{5,4},{6,7},{7,6},{8,9},{9,8},{10,11... | collective-permute-start | bytes 1572872 | tf_op jit(solution)/shard_map/ppermute | solution.py:183
  45.5 21.9 %collective-permute-start.7 = (bf16[1024,256]{1,0:T(8,128)(2,1)S(1)}, bf16[1024,256]{1,0:T(8,128)(2,1)S(1)}, u32[]{:S(2)}, u32[]{:S(2)}) collective-permute-start(bf16[1024,256]{1,0:T(8,128)(2,1)S(1)} %collective-permute-done.6.refs_2_), channel_id=1, source_target_pairs={{0,1},{1,0},{2,3},{3,2},{4,5},{5,4},{6,7},{7,6},{8,9},{9,8},{10,11... | collective-permute-start | bytes 1572872 | tf_op jit(solution)/shard_map/ppermute | solution.py:183
  45.9 21.5 %collective-permute-start.9 = (bf16[1024,256]{1,0:T(8,128)(2,1)S(1)}, bf16[1024,256]{1,0:T(8,128)(2,1)S(1)}, u32[]{:S(2)}, u32[]{:S(2)}) collective-permute-start(bf16[1024,256]{1,0:T(8,128)(2,1)S(1)} %collective-permute-done.8.refs_4_), channel_id=1, source_target_pairs={{0,1},{1,0},{2,3},{3,2},{4,5},{5,4},{6,7},{7,6},{8,9},{9,8},{10,11... | collective-permute-start | bytes 1572872 | tf_op jit(solution)/shard_map/ppermute | solution.py:183
  46.0 21.4 %collective-permute-start.11 = (bf16[1024,256]{1,0:T(8,128)(2,1)S(1)}, bf16[1024,256]{1,0:T(8,128)(2,1)S(1)}, u32[]{:S(2)}, u32[]{:S(2)}) collective-permute-start(bf16[1024,256]{1,0:T(8,128)(2,1)S(1)} %collective-permute-done.10.refs_6_), channel_id=1, source_target_pairs={{0,1},{1,0},{2,3},{3,2},{4,5},{5,4},{6,7},{7,6},{8,9},{9,8},{10,11... | collective-permute-start | bytes 1572872 | tf_op jit(solution)/shard_map/ppermute | solution.py:183
  65.8 9.2 %collective-permute-start.20 = (bf16[2,512,256]{2,1,0:T(8,128)(2,1)S(1)}, bf16[2,512,256]{2,1,0:T(8,128)(2,1)S(1)}, u32[]{:S(2)}, u32[]{:S(2)}) collective-permute-start(bf16[2,512,256]{2,1,0:T(8,128)(2,1)S(1)} %project.7), channel_id=1, source_target_pairs={{0,8},{1,17},{2,10},{3,19},{4,12},{5,21},{6,14},{7,23},{8,0},{9,25... | collective-permute-start | bytes 1572872 | tf_op jit(solution)/shard_map/ppermute | solution.py:183
  69.0 14.5 %collective-permute-start.12 = (bf16[2,512,256]{2,1,0:T(8,128)(2,1)S(1)}, bf16[2,512,256]{2,1,0:T(8,128)(2,1)S(1)}, u32[]{:S(2)}, u32[]{:S(2)}) collective-permute-start(bf16[2,512,256]{2,1,0:T(8,128)(2,1)S(1)} %project.5), channel_id=1, source_target_pairs={{0,8},{1,17},{2,10},{3,19},{4,12},{5,21},{6,14},{7,23},{8,0},{9,25... | collective-permute-start | bytes 1572872 | tf_op jit(solution)/shard_map/ppermute | solution.py:183
  75.1 10.0 %collective-permute-start.21 = (bf16[512,256]{1,0:T(8,128)(2,1)S(1)}, bf16[512,256]{1,0:T(8,128)(2,1)S(1)}, u32[]{:S(2)}, u32[]{:S(2)}) collective-permute-start(bf16[512,256]{1,0:T(8,128)(2,1)S(1)} %fusion.3), channel_id=1, source_target_pairs={{0,16},{1,9},{2,18},{3,11},{4,20},{5,13},{6,22},{7,15},{8,24},{9,1... | collective-permute-start | bytes 786440 | tf_op jit(solution)/shard_map/ppermute | solution.py:183
  83.5 6.4 %collective-permute-start.13 = (bf16[512,256]{1,0:T(8,128)(2,1)S(1)}, bf16[512,256]{1,0:T(8,128)(2,1)S(1)}, u32[]{:S(2)}, u32[]{:S(2)}) collective-permute-start(bf16[512,256]{1,0:T(8,128)(2,1)S(1)} %fusion.2), channel_id=1, source_target_pairs={{0,16},{1,9},{2,18},{3,11},{4,20},{5,13},{6,22},{7,15},{8,24},{9,1... | collective-permute-start | bytes 786440 | tf_op jit(solution)/shard_map/ppermute | solution.py:183
  (1 other events, 3.7 us)

commit v4 on v3

--- a/solution.py
+++ b/solution.py
@@ -138,41 +138,40 @@
 
 
 def project(attended, pieces, half, first_slot, slots):
-    tokens, depth = attended.shape
+    tokens, _ = attended.shape
     width = pieces[0].shape[1]
 
     def body(left, *refs):
-        sources = refs[: len(pieces)]
-        out, rights, sems = refs[len(pieces) :]
+        sources, out = refs[:-1], refs[-1]
         shard = lax.axis_index("docs")
         group = lax.axis_index("heads")
         odd = lax.rem(shard, 2)
         plane = lax.div(shard, 2)
-        early = jnp.where(odd == 1, 2, 1)
+        early = jnp.where(odd == half, 2, 1)
         late = 3 - early
-        targets = [group ^ early, group ^ 3, group, group ^ late]
-        for slot, target in enumerate(targets[first_slot : first_slot + slots]):
+        targets = [group ^ early, group ^ 3, group, group ^ late][first_slot : first_slot + slots]
+
+        def one_slot(slot, carry):
+            target = jnp.where(slot == 0, targets[0], targets[1])
             distance = jnp.abs(plane - target)
-            below = jnp.where(target < plane, 1, 0)
-            away = 2 * distance + (below ^ odd)
+            arrived_on_odd = jnp.where((target < plane) | (distance > 1), 1, 0)
+            away = 2 * distance + (arrived_on_odd ^ odd)
             index = jnp.where(distance == 0, odd ^ half, away)
             for j, source in enumerate(sources):
                 @pl.when(index == j)
-                def _(source=source, slot=slot):
-                    pltpu.make_async_copy(source, rights.at[slot], sems.at[slot]).start()
-        for slot in range(slots):
-            pltpu.make_async_copy(sources[0], rights.at[slot], sems.at[slot]).wait()
-            out[slot] = jnp.dot(
-                left[...], rights[slot], preferred_element_type=jnp.float32
-            ).astype(jnp.bfloat16)
-
-    shape = jax.ShapeDtypeStruct((slots, tokens, width), jnp.bfloat16)
+                def _(source=source):
+                    out[slot] = jnp.dot(
+                        left[...], source[...], preferred_element_type=jnp.float32
+                    ).astype(jnp.bfloat16)
+            return carry
+
+        lax.fori_loop(0, slots, one_slot, 0)
+
     return pl.pallas_call(
         body,
-        out_shape=shape,
-        in_specs=[VMEM] + [ANY] * len(pieces),
+        out_shape=jax.ShapeDtypeStruct((slots, tokens, width), jnp.bfloat16),
+        in_specs=[VMEM] * (1 + len(pieces)),
         out_specs=VMEM,
-        scratch_shapes=[pltpu.VMEM((slots, depth, width), jnp.bfloat16), pltpu.SemaphoreType.DMA((slots,))],
         compiler_params=pltpu.CompilerParams(vmem_limit_bytes=16 << 20),
         name="project",
     )(attended, *pieces)
@@ -194,7 +193,7 @@
             if p >= step - 1:
                 route.append((2 * p + (step > 1), 2 * p + 3))
             if p + 1 <= planes - step:
-                route.append((2 * p + 2 + (step == 1), 2 * p))
+                route.append((2 * p + 2 + (step != 2), 2 * p + (step > 1)))
         return route
 
     def exchange(block, early):
@@ -240,15 +239,17 @@
         results = []
         for half in range(2):
             outward = project(attended, pieces[half], half, 0, 2)
-            arrived = exchange(outward, True)
+            arrived = exchange(outward, half == 1)
             keep = project(attended, pieces[half], half, 2, 2)
             onward = (keep[1].astype(f32) + arrived[1].astype(f32)).astype(jnp.bfloat16)
-            final = exchange(onward, False)
+            final = exchange(onward, half == 0)
             results.append((keep[0].astype(f32) + arrived[0].astype(f32) + final.astype(f32)).astype(jnp.bfloat16))
-        ahead = lax.axis_index("heads") > lax.axis_index("docs") // 2
-        return jnp.concatenate(
-            [jnp.where(ahead, results[1], results[0]), jnp.where(ahead, results[0], results[1])], axis=1
-        )
+        half_width = results[0].shape[1]
+        ahead = (lax.axis_index("heads") > lax.axis_index("docs") // 2).astype(jnp.int32)
+        mixed = jnp.zeros((results[0].shape[0], 2 * half_width), jnp.bfloat16)
+        mixed = lax.dynamic_update_slice(mixed, results[0], (0, ahead * half_width))
+        mixed = lax.optimization_barrier(mixed)
+        return lax.dynamic_update_slice(mixed, results[1], (0, (1 - ahead) * half_width))
 
     return local
 

time: 91.9 us -> 90.9 us (0.989)
  starting transfers between devices: 34.5 us -> 38.8 us
  waiting for transfers between devices: 33.7 us -> 30.5 us
  Pallas kernels: 20.4 us -> 18 us
    ppermute x22, starting transfers between devices: 34.5 us -> 38.8 us  [send(): return lax.ppermute(block, axis, route)]
    ppermute x22, waiting for transfers between devices: 33.7 us -> 30.5 us  [send(): return lax.ppermute(block, axis, route)]
    pallas_call x4, Pallas kernels: 6.21 us -> 3.81 us  [project(): pl.pallas_call(body, out_shape=jax.ShapeDtypeStruct((slots, tokens, width...]
  transfers between devices with their start and end apart: 22 -> 22, of which waited for: 8 -> 8; matrix products, arithmetic and copies ran while one was open for 1% -> 1% of each run, Pallas kernels for 22% -> 20%
where the time goes in v4:
time: 90.9 us; the launch traced here: 90 us
  starting transfers between devices  38.8 us (43%)
  waiting for transfers between devices  30.5 us (34%)
  Pallas kernels  18 us (20%)
  other arithmetic  2.02 us (2%)
    ppermute x22, starting transfers between devices, send(): return lax.ppermute(block, axis, route)  38.8 us
    ppermute x22, waiting for transfers between devices, send(): return lax.ppermute(block, axis, route)  30.5 us
    pallas_call x4, Pallas kernels, attention(): pl.pallas_call(functools.partial(attend, first=part, heads_together=toget...  13.9 us
    pallas_call x4, Pallas kernels, project(): pl.pallas_call(body, out_shape=jax.ShapeDtypeStruct((slots, tokens, width...  3.81 us
  transfers between devices with their start and end apart: 22, of which 8 were waited for; matrix products, arithmetic and copies ran while one was open for 1% of the time, Pallas kernels for 20%

profile of v4, /device:TPU:16, one launch (start us, length us, event | category | flops | bytes accessed | tf_op | source)
XLA Modules:
  0.0 90.0 jit_solution(6549829202260511750)
XLA Ops:
  0.0 3.6 %collective-permute-start.6 = (bf16[1024,256]{1,0:T(8,128)(2,1)}, bf16[1024,256]{1,0:T(8,128)(2,1)S(1)}, u32[]{:S(2)}, u32[]{:S(2)}) collective-permute-start(bf16[1024,256]{1,0:T(8,128)(2,1)} %refs_0_.7), channel_id=1, source_target_pairs={{0,3},{3,0},{2,5},{5,2},{4,7},{7,4},{8,11},{11,8},{10,13},{13,10},... | collective-permute-start | bytes 1572872 | tf_op jit(solution)/shard_map/ppermute | solution.py:182
  3.6 2.1 %collective-permute-start.14 = (bf16[1024,256]{1,0:T(8,128)(2,1)S(1)}, bf16[1024,256]{1,0:T(8,128)(2,1)S(1)}, u32[]{:S(2)}, u32[]{:S(2)}) collective-permute-start(bf16[1024,256]{1,0:T(8,128)(2,1)S(1)} %collective-permute-done.5.refs_1_), channel_id=1, source_target_pairs={{0,3},{3,0},{2,5},{5,2},{4,7},{7,4},{8,11},{11,8},{10,13},{13,10},... | collective-permute-start | bytes 1572872 | tf_op jit(solution)/shard_map/ppermute | solution.py:182
  5.7 5.1 %collective-permute-done.6.refs_2_ = bf16[1024,256]{1,0:T(8,128)(2,1)S(1)} collective-permute-done((bf16[1024,256]{1,0:T(8,128)(2,1)}, bf16[1024,256]{1,0:T(8,128)(2,1)S(1)}, u32[]{:S(2)}, u32[]{:S(2)}) %collective-permute-start.6) | collective-permute-done | bytes 524320 | tf_op jit(solution)/shard_map/ppermute | solution.py:182
  10.9 2.6 %collective-permute-start.8 = (bf16[1024,256]{1,0:T(8,128)(2,1)S(1)}, bf16[1024,256]{1,0:T(8,128)(2,1)S(1)}, u32[]{:S(2)}, u32[]{:S(2)}) collective-permute-start(bf16[1024,256]{1,0:T(8,128)(2,1)S(1)} %collective-permute-done.6.refs_2_), channel_id=1, source_target_pairs={{2,1},{3,5},{4,3},{5,7},{10,9},{11,13},{12,11},{13,15},{18,17},{19... | collective-permute-start | bytes 1572872 | tf_op jit(solution)/shard_map/ppermute | solution.py:182
  13.5 3.9 %collective-permute-done.14.refs_2_ = bf16[1024,256]{1,0:T(8,128)(2,1)S(1)} collective-permute-done((bf16[1024,256]{1,0:T(8,128)(2,1)S(1)}, bf16[1024,256]{1,0:T(8,128)(2,1)S(1)}, u32[]{:S(2)}, u32[]{:S(2)}) %collective-permute-start.14) | collective-permute-done | bytes 524320 | tf_op jit(solution)/shard_map/ppermute | solution.py:182
  17.4 1.4 %collective-permute-start.16 = (bf16[1024,256]{1,0:T(8,128)(2,1)S(1)}, bf16[1024,256]{1,0:T(8,128)(2,1)S(1)}, u32[]{:S(2)}, u32[]{:S(2)}) collective-permute-start(bf16[1024,256]{1,0:T(8,128)(2,1)S(1)} %collective-permute-done.14.refs_2_), channel_id=1, source_target_pairs={{2,1},{3,5},{4,3},{5,7},{10,9},{11,13},{12,11},{13,15},{18,17},{19... | collective-permute-start | bytes 1572872 | tf_op jit(solution)/shard_map/ppermute | solution.py:182
  19.8 1.9 %collective-permute-start.1 = (bf16[2,512,128]{2,1,0:T(8,128)(2,1)S(1)}, bf16[2,512,128]{2,1,0:T(8,128)(2,1)S(1)}, u32[]{:S(2)}, u32[]{:S(2)}) collective-permute-start(bf16[2,512,128]{2,1,0:T(8,128)(2,1)S(1)} %pad_maximum_fusion.own), channel_id=1, source_target_pairs={{0,2},{1,3},{2,4},{3,5},{4,6},{5,7},{8,10},{9,11},{10,12},{11,13},... | collective-permute-start | bytes 786440 | tf_op jit(solution)/shard_map/ppermute | solution.py:182
  21.7 2.6 %collective-permute-start = (bf16[2,512,128]{2,1,0:T(8,128)(2,1)S(1)}, bf16[2,512,128]{2,1,0:T(8,128)(2,1)S(1)}, u32[]{:S(2)}, u32[]{:S(2)}) collective-permute-start(bf16[2,512,128]{2,1,0:T(8,128)(2,1)S(1)} %pad_maximum_fusion.own), channel_id=1, source_target_pairs={{0,1},{1,0},{2,3},{3,2},{4,5},{5,4},{6,7},{7,6},{8,9},{9,8},{10,11... | collective-permute-start | bytes 786440 | tf_op jit(solution)/shard_map/ppermute | solution.py:182
  25.0 5.9 %collective-permute-done.1.near = bf16[2,512,128]{2,1,0:T(8,128)(2,1)S(1)} collective-permute-done((bf16[2,512,128]{2,1,0:T(8,128)(2,1)S(1)}, bf16[2,512,128]{2,1,0:T(8,128)(2,1)S(1)}, u32[]{:S(2)}, u32[]{:S(2)}) %collective-permute-start.1) | collective-permute-done | bytes 262176 | tf_op jit(solution)/shard_map/ppermute | solution.py:182
  30.9 1.9 %collective-permute-start.3 = (bf16[2,512,128]{2,1,0:T(8,128)(2,1)S(1)}, bf16[2,512,128]{2,1,0:T(8,128)(2,1)S(1)}, u32[]{:S(2)}, u32[]{:S(2)}) collective-permute-start(bf16[2,512,128]{2,1,0:T(8,128)(2,1)S(1)} %collective-permute-done.1.near), channel_id=1, source_target_pairs={{2,4},{3,5},{4,6},{5,7},{10,12},{11,13},{12,14},{13,15},{18,20},{1... | collective-permute-start | bytes 786440 | tf_op jit(solution)/shard_map/ppermute | solution.py:182
  32.8 4.1 %collective-permute-start.7 = (bf16[1024,256]{1,0:T(8,128)(2,1)S(1)}, bf16[1024,256]{1,0:T(8,128)(2,1)S(1)}, u32[]{:S(2)}, u32[]{:S(2)}) collective-permute-start(bf16[1024,256]{1,0:T(8,128)(2,1)S(1)} %collective-permute-done.6.refs_2_), channel_id=1, source_target_pairs={{0,1},{1,0},{2,3},{3,2},{4,5},{5,4},{6,7},{7,6},{8,9},{9,8},{10,11... | collective-permute-start | bytes 1572872 | tf_op jit(solution)/shard_map/ppermute | solution.py:182
  38.4 1.7 %collective-permute-done.3.far = bf16[2,512,128]{2,1,0:T(8,128)(2,1)S(1)} collective-permute-done((bf16[2,512,128]{2,1,0:T(8,128)(2,1)S(1)}, bf16[2,512,128]{2,1,0:T(8,128)(2,1)S(1)}, u32[]{:S(2)}, u32[]{:S(2)}) %collective-permute-start.3) | collective-permute-done | bytes 262176 | tf_op jit(solution)/shard_map/ppermute | solution.py:182
  40.1 4.2 %collective-permute-start.4 = (bf16[2,512,128]{2,1,0:T(8,128)(2,1)S(1)}, bf16[2,512,128]{2,1,0:T(8,128)(2,1)S(1)}, u32[]{:S(2)}, u32[]{:S(2)}) collective-permute-start(bf16[2,512,128]{2,1,0:T(8,128)(2,1)S(1)} %collective-permute-done.3.far), channel_id=1, source_target_pairs={{0,1},{1,0},{2,3},{3,2},{4,5},{5,4},{6,7},{7,6},{8,9},{9,8},{10,11... | collective-permute-start | bytes 786440 | tf_op jit(solution)/shard_map/ppermute | solution.py:182
  46.0 3.9 %collective-permute-start.19 = (bf16[1024,256]{1,0:T(8,128)(2,1)S(1)}, bf16[1024,256]{1,0:T(8,128)(2,1)S(1)}, u32[]{:S(2)}, u32[]{:S(2)}) collective-permute-start(bf16[1024,256]{1,0:T(8,128)(2,1)S(1)} %collective-permute-done.18.refs_6_), channel_id=1, source_target_pairs={{0,1},{1,0},{2,3},{3,2},{4,5},{5,4},{6,7},{7,6},{8,9},{9,8},{10,11... | collective-permute-start | bytes 1572872 | tf_op jit(solution)/shard_map/ppermute | solution.py:182
  50.2 3.4 %attend.4.refs_0_ = bf16[512,1024]{1,0:T(8,128)(2,1)S(1)} custom-call(s32[4]{0:T(128)S(1)} %copy-done.2, bf16[512,1024]{1,0:T(8,128)(2,1)S(1)} %copy-done, bf16[3072,128]{1,0:T(8,128)(2,1)S(1)} %get-tuple-element.7.keys, bf16[3072,256]{1,0:T(8,128)(2,1)S(1)} %get-tuple-element.8.values), custom_call_target="tpu_custom_call" | custom-call | tf_op jit(solution)/shard_map/attend/pallas_call | solution.py:125
  53.7 3.4 %attend.5.refs_0_ = bf16[512,1024]{1,0:T(8,128)(2,1)S(1)} custom-call(s32[4]{0:T(128)S(1)} %copy-done.2, bf16[512,1024]{1,0:T(8,128)(2,1)S(1)} %copy-done, bf16[3072,128]{1,0:T(8,128)(2,1)S(1)} %get-tuple-element.7.keys, bf16[3072,256]{1,0:T(8,128)(2,1)S(1)} %get-tuple-element.8.values, ...), custom_call_target="tpu_custom_call", output_to_operand_aliasing={{}: (4, {})} | custom-call | tf_op jit(solution)/shard_map/attend/pallas_call | solution.py:125
  57.1 3.4 %attend.6.refs_0_ = bf16[512,1024]{1,0:T(8,128)(2,1)S(1)} custom-call(s32[4]{0:T(128)S(1)} %copy-done.2, bf16[512,1024]{1,0:T(8,128)(2,1)S(1)} %copy-done, bf16[3072,128]{1,0:T(8,128)(2,1)S(1)} %get-tuple-element.7.keys, bf16[3072,256]{1,0:T(8,128)(2,1)S(1)} %get-tuple-element.8.values, ...), custom_call_target="tpu_custom_call", output_to_operand_aliasing={{}: (4, {})} | custom-call | tf_op jit(solution)/shard_map/attend/pallas_call | solution.py:125
  60.5 3.6 %attend.7.left = bf16[512,1024]{1,0:T(8,128)(2,1)S(1)} custom-call(s32[4]{0:T(128)S(1)} %copy-done.2, bf16[512,1024]{1,0:T(8,128)(2,1)S(1)} %copy-done, bf16[3072,128]{1,0:T(8,128)(2,1)S(1)} %get-tuple-element.7.keys, bf16[3072,256]{1,0:T(8,128)(2,1)S(1)} %get-tuple-element.8.values, bf16[512,1024]{1,0:T(8,128)(2,1)S(1)} %attend.6.refs_0_), custom_call_target="tpu_custom_call", output_to_operand_aliasing={{}: (4, {})} | custom-call | tf_op jit(solution)/shard_map/attend/pallas_call | solution.py:125
  65.2 1.6 %collective-permute-start.12 = (bf16[2,512,256]{2,1,0:T(8,128)(2,1)S(1)}, bf16[2,512,256]{2,1,0:T(8,128)(2,1)S(1)}, u32[]{:S(2)}, u32[]{:S(2)}) collective-permute-start(bf16[2,512,256]{2,1,0:T(8,128)(2,1)S(1)} %project.5), channel_id=1, source_target_pairs={{0,16},{1,9},{2,18},{3,11},{4,20},{5,13},{6,22},{7,15},{8,24},{9,1... | collective-permute-start | bytes 1572872 | tf_op jit(solution)/shard_map/ppermute | solution.py:182
  67.8 1.5 %collective-permute-start.20 = (bf16[2,512,256]{2,1,0:T(8,128)(2,1)S(1)}, bf16[2,512,256]{2,1,0:T(8,128)(2,1)S(1)}, u32[]{:S(2)}, u32[]{:S(2)}) collective-permute-start(bf16[2,512,256]{2,1,0:T(8,128)(2,1)S(1)} %project.7), channel_id=1, source_target_pairs={{0,8},{1,17},{2,10},{3,19},{4,12},{5,21},{6,14},{7,23},{8,0},{9,25... | collective-permute-start | bytes 1572872 | tf_op jit(solution)/shard_map/ppermute | solution.py:182
  70.3 8.5 %collective-permute-done.12 = bf16[2,512,256]{2,1,0:T(8,128)(2,1)S(1)} collective-permute-done((bf16[2,512,256]{2,1,0:T(8,128)(2,1)S(1)}, bf16[2,512,256]{2,1,0:T(8,128)(2,1)S(1)}, u32[]{:S(2)}, u32[]{:S(2)}) %collective-permute-start.12) | collective-permute-done | bytes 524320 | tf_op jit(solution)/shard_map/ppermute | solution.py:182
  78.8 2.5 %collective-permute-start.13 = (bf16[512,256]{1,0:T(8,128)(2,1)S(1)}, bf16[512,256]{1,0:T(8,128)(2,1)S(1)}, u32[]{:S(2)}, u32[]{:S(2)}) collective-permute-start(bf16[512,256]{1,0:T(8,128)(2,1)S(1)} %fusion.2), channel_id=1, source_target_pairs={{0,8},{1,17},{2,10},{3,19},{4,12},{5,21},{6,14},{7,23},{8,0},{9,25... | collective-permute-start | bytes 786440 | tf_op jit(solution)/shard_map/ppermute | solution.py:182
  82.4 1.6 %collective-permute-start.21 = (bf16[512,256]{1,0:T(8,128)(2,1)S(1)}, bf16[512,256]{1,0:T(8,128)(2,1)S(1)}, u32[]{:S(2)}, u32[]{:S(2)}) collective-permute-start(bf16[512,256]{1,0:T(8,128)(2,1)S(1)} %fusion.3), channel_id=1, source_target_pairs={{0,16},{1,9},{2,18},{3,11},{4,20},{5,13},{6,22},{7,15},{8,24},{9,1... | collective-permute-start | bytes 786440 | tf_op jit(solution)/shard_map/ppermute | solution.py:182
  83.9 4.3 %collective-permute-done.13 = bf16[512,256]{1,0:T(8,128)(2,1)S(1)} collective-permute-done((bf16[512,256]{1,0:T(8,128)(2,1)S(1)}, bf16[512,256]{1,0:T(8,128)(2,1)S(1)}, u32[]{:S(2)}, u32[]{:S(2)}) %collective-permute-start.13) | collective-permute-done | bytes 262176 | tf_op jit(solution)/shard_map/ppermute | solution.py:182
  (43 shorter events, 10.7 us)
Async XLA Ops:
  0.0 50.2 %copy-start.2 = (s32[4]{0:T(128)S(1)}, s32[4]{0:T(128)}, u32[]{:S(2)}) copy-start(s32[4]{0:T(128)} %docs.7) | copy-start | bytes 52
  0.0 50.2 %copy-start = (bf16[512,1024]{1,0:T(8,128)(2,1)S(1)}, bf16[512,1024]{1,0:T(8,128)(2,1)}, u32[]{:S(2)}) copy-start(bf16[512,1024]{1,0:T(8,128)(2,1)} %query.7) | copy-start | bytes 3145732
  0.0 3.6 %collective-permute-start.5 = (bf16[1024,256]{1,0:T(8,128)(2,1)}, bf16[1024,256]{1,0:T(8,128)(2,1)S(1)}, u32[]{:S(2)}, u32[]{:S(2)}) collective-permute-start(bf16[1024,256]{1,0:T(8,128)(2,1)} %refs_0_.7), channel_id=1, source_target_pairs={{0,1},{1,0},{2,3},{3,2},{4,5},{5,4},{6,7},{7,6},{8,9},{9,8},{10,11... | collective-permute-start | bytes 1572872 | tf_op jit(solution)/shard_map/ppermute | solution.py:182
  0.0 10.8 %collective-permute-start.6 = (bf16[1024,256]{1,0:T(8,128)(2,1)}, bf16[1024,256]{1,0:T(8,128)(2,1)S(1)}, u32[]{:S(2)}, u32[]{:S(2)}) collective-permute-start(bf16[1024,256]{1,0:T(8,128)(2,1)} %refs_0_.7), channel_id=1, source_target_pairs={{0,3},{3,0},{2,5},{5,2},{4,7},{7,4},{8,11},{11,8},{10,13},{13,10},... | collective-permute-start | bytes 1572872 | tf_op jit(solution)/shard_map/ppermute | solution.py:182
  3.6 13.8 %collective-permute-start.14 = (bf16[1024,256]{1,0:T(8,128)(2,1)S(1)}, bf16[1024,256]{1,0:T(8,128)(2,1)S(1)}, u32[]{:S(2)}, u32[]{:S(2)}) collective-permute-start(bf16[1024,256]{1,0:T(8,128)(2,1)S(1)} %collective-permute-done.5.refs_1_), channel_id=1, source_target_pairs={{0,3},{3,0},{2,5},{5,2},{4,7},{7,4},{8,11},{11,8},{10,13},{13,10},... | collective-permute-start | bytes 1572872 | tf_op jit(solution)/shard_map/ppermute | solution.py:182
  10.9 13.5 %collective-permute-start.8 = (bf16[1024,256]{1,0:T(8,128)(2,1)S(1)}, bf16[1024,256]{1,0:T(8,128)(2,1)S(1)}, u32[]{:S(2)}, u32[]{:S(2)}) collective-permute-start(bf16[1024,256]{1,0:T(8,128)(2,1)S(1)} %collective-permute-done.6.refs_2_), channel_id=1, source_target_pairs={{2,1},{3,5},{4,3},{5,7},{10,9},{11,13},{12,11},{13,15},{18,17},{19... | collective-permute-start | bytes 1572872 | tf_op jit(solution)/shard_map/ppermute | solution.py:182
  17.4 19.5 %collective-permute-start.16 = (bf16[1024,256]{1,0:T(8,128)(2,1)S(1)}, bf16[1024,256]{1,0:T(8,128)(2,1)S(1)}, u32[]{:S(2)}, u32[]{:S(2)}) collective-permute-start(bf16[1024,256]{1,0:T(8,128)(2,1)S(1)} %collective-permute-done.14.refs_2_), channel_id=1, source_target_pairs={{2,1},{3,5},{4,3},{5,7},{10,9},{11,13},{12,11},{13,15},{18,17},{19... | collective-permute-start | bytes 1572872 | tf_op jit(solution)/shard_map/ppermute | solution.py:182
  19.8 11.1 %collective-permute-start.1 = (bf16[2,512,128]{2,1,0:T(8,128)(2,1)S(1)}, bf16[2,512,128]{2,1,0:T(8,128)(2,1)S(1)}, u32[]{:S(2)}, u32[]{:S(2)}) collective-permute-start(bf16[2,512,128]{2,1,0:T(8,128)(2,1)S(1)} %pad_maximum_fusion.own), channel_id=1, source_target_pairs={{0,2},{1,3},{2,4},{3,5},{4,6},{5,7},{8,10},{9,11},{10,12},{11,13},... | collective-permute-start | bytes 786440 | tf_op jit(solution)/shard_map/ppermute | solution.py:182
  21.7 15.9 %collective-permute-start = (bf16[2,512,128]{2,1,0:T(8,128)(2,1)S(1)}, bf16[2,512,128]{2,1,0:T(8,128)(2,1)S(1)}, u32[]{:S(2)}, u32[]{:S(2)}) collective-permute-start(bf16[2,512,128]{2,1,0:T(8,128)(2,1)S(1)} %pad_maximum_fusion.own), channel_id=1, source_target_pairs={{0,1},{1,0},{2,3},{3,2},{4,5},{5,4},{6,7},{7,6},{8,9},{9,8},{10,11... | collective-permute-start | bytes 786440 | tf_op jit(solution)/shard_map/ppermute | solution.py:182
  24.3 20.0 %collective-permute-start.10 = (bf16[1024,256]{1,0:T(8,128)(2,1)S(1)}, bf16[1024,256]{1,0:T(8,128)(2,1)S(1)}, u32[]{:S(2)}, u32[]{:S(2)}) collective-permute-start(bf16[1024,256]{1,0:T(8,128)(2,1)S(1)} %collective-permute-done.8.refs_4_), channel_id=1, source_target_pairs={{3,1},{5,7},{11,9},{13,15},{19,17},{21,23},{27,25},{29,31}} | collective-permute-start | bytes 1572872 | tf_op jit(solution)/shard_map/ppermute | solution.py:182
  30.9 9.2 %collective-permute-start.3 = (bf16[2,512,128]{2,1,0:T(8,128)(2,1)S(1)}, bf16[2,512,128]{2,1,0:T(8,128)(2,1)S(1)}, u32[]{:S(2)}, u32[]{:S(2)}) collective-permute-start(bf16[2,512,128]{2,1,0:T(8,128)(2,1)S(1)} %collective-permute-done.1.near), channel_id=1, source_target_pairs={{2,4},{3,5},{4,6},{5,7},{10,12},{11,13},{12,14},{13,15},{18,20},{1... | collective-permute-start | bytes 786440 | tf_op jit(solution)/shard_map/ppermute | solution.py:182
  32.8 13.0 %collective-permute-start.7 = (bf16[1024,256]{1,0:T(8,128)(2,1)S(1)}, bf16[1024,256]{1,0:T(8,128)(2,1)S(1)}, u32[]{:S(2)}, u32[]{:S(2)}) collective-permute-start(bf16[1024,256]{1,0:T(8,128)(2,1)S(1)} %collective-permute-done.6.refs_2_), channel_id=1, source_target_pairs={{0,1},{1,0},{2,3},{3,2},{4,5},{5,4},{6,7},{7,6},{8,9},{9,8},{10,11... | collective-permute-start | bytes 1572872 | tf_op jit(solution)/shard_map/ppermute | solution.py:182
  37.0 9.0 %collective-permute-start.18 = (bf16[1024,256]{1,0:T(8,128)(2,1)S(1)}, bf16[1024,256]{1,0:T(8,128)(2,1)S(1)}, u32[]{:S(2)}, u32[]{:S(2)}) collective-permute-start(bf16[1024,256]{1,0:T(8,128)(2,1)S(1)} %collective-permute-done.16.refs_4_), channel_id=1, source_target_pairs={{3,1},{5,7},{11,9},{13,15},{19,17},{21,23},{27,25},{29,31}} | collective-permute-start | bytes 1572872 | tf_op jit(solution)/shard_map/ppermute | solution.py:182
  37.7 6.7 %collective-permute-start.2 = (bf16[2,512,128]{2,1,0:T(8,128)(2,1)S(1)}, bf16[2,512,128]{2,1,0:T(8,128)(2,1)S(1)}, u32[]{:S(2)}, u32[]{:S(2)}) collective-permute-start(bf16[2,512,128]{2,1,0:T(8,128)(2,1)S(1)} %collective-permute-done.1.near), channel_id=1, source_target_pairs={{0,1},{1,0},{2,3},{3,2},{4,5},{5,4},{6,7},{7,6},{8,9},{9,8},{10,11... | collective-permute-start | bytes 786440 | tf_op jit(solution)/shard_map/ppermute | solution.py:182
  40.1 5.3 %collective-permute-start.4 = (bf16[2,512,128]{2,1,0:T(8,128)(2,1)S(1)}, bf16[2,512,128]{2,1,0:T(8,128)(2,1)S(1)}, u32[]{:S(2)}, u32[]{:S(2)}) collective-permute-start(bf16[2,512,128]{2,1,0:T(8,128)(2,1)S(1)} %collective-permute-done.3.far), channel_id=1, source_target_pairs={{0,1},{1,0},{2,3},{3,2},{4,5},{5,4},{6,7},{7,6},{8,9},{9,8},{10,11... | collective-permute-start | bytes 786440 | tf_op jit(solution)/shard_map/ppermute | solution.py:182
  44.3 19.9 %collective-permute-start.9 = (bf16[1024,256]{1,0:T(8,128)(2,1)S(1)}, bf16[1024,256]{1,0:T(8,128)(2,1)S(1)}, u32[]{:S(2)}, u32[]{:S(2)}) collective-permute-start(bf16[1024,256]{1,0:T(8,128)(2,1)S(1)} %collective-permute-done.8.refs_4_), channel_id=1, source_target_pairs={{0,1},{1,0},{2,3},{3,2},{4,5},{5,4},{6,7},{7,6},{8,9},{9,8},{10,11... | collective-permute-start | bytes 1572872 | tf_op jit(solution)/shard_map/ppermute | solution.py:182
  44.3 19.9 %collective-permute-start.11 = (bf16[1024,256]{1,0:T(8,128)(2,1)S(1)}, bf16[1024,256]{1,0:T(8,128)(2,1)S(1)}, u32[]{:S(2)}, u32[]{:S(2)}) collective-permute-start(bf16[1024,256]{1,0:T(8,128)(2,1)S(1)} %collective-permute-done.10.refs_6_), channel_id=1, source_target_pairs={{0,1},{1,0},{2,3},{3,2},{4,5},{5,4},{6,7},{7,6},{8,9},{9,8},{10,11... | collective-permute-start | bytes 1572872 | tf_op jit(solution)/shard_map/ppermute | solution.py:182
  45.5 21.3 %collective-permute-start.15 = (bf16[1024,256]{1,0:T(8,128)(2,1)S(1)}, bf16[1024,256]{1,0:T(8,128)(2,1)S(1)}, u32[]{:S(2)}, u32[]{:S(2)}) collective-permute-start(bf16[1024,256]{1,0:T(8,128)(2,1)S(1)} %collective-permute-done.14.refs_2_), channel_id=1, source_target_pairs={{0,1},{1,0},{2,3},{3,2},{4,5},{5,4},{6,7},{7,6},{8,9},{9,8},{10,11... | collective-permute-start | bytes 1572872 | tf_op jit(solution)/shard_map/ppermute | solution.py:182
  45.9 20.9 %collective-permute-start.17 = (bf16[1024,256]{1,0:T(8,128)(2,1)S(1)}, bf16[1024,256]{1,0:T(8,128)(2,1)S(1)}, u32[]{:S(2)}, u32[]{:S(2)}) collective-permute-start(bf16[1024,256]{1,0:T(8,128)(2,1)S(1)} %collective-permute-done.16.refs_4_), channel_id=1, source_target_pairs={{0,1},{1,0},{2,3},{3,2},{4,5},{5,4},{6,7},{7,6},{8,9},{9,8},{10,11... | collective-permute-start | bytes 1572872 | tf_op jit(solution)/shard_map/ppermute | solution.py:182
  46.0 20.8 %collective-permute-start.19 = (bf16[1024,256]{1,0:T(8,128)(2,1)S(1)}, bf16[1024,256]{1,0:T(8,128)(2,1)S(1)}, u32[]{:S(2)}, u32[]{:S(2)}) collective-permute-start(bf16[1024,256]{1,0:T(8,128)(2,1)S(1)} %collective-permute-done.18.refs_6_), channel_id=1, source_target_pairs={{0,1},{1,0},{2,3},{3,2},{4,5},{5,4},{6,7},{7,6},{8,9},{9,8},{10,11... | collective-permute-start | bytes 1572872 | tf_op jit(solution)/shard_map/ppermute | solution.py:182
  65.2 13.6 %collective-permute-start.12 = (bf16[2,512,256]{2,1,0:T(8,128)(2,1)S(1)}, bf16[2,512,256]{2,1,0:T(8,128)(2,1)S(1)}, u32[]{:S(2)}, u32[]{:S(2)}) collective-permute-start(bf16[2,512,256]{2,1,0:T(8,128)(2,1)S(1)} %project.5), channel_id=1, source_target_pairs={{0,16},{1,9},{2,18},{3,11},{4,20},{5,13},{6,22},{7,15},{8,24},{9,1... | collective-permute-start | bytes 1572872 | tf_op jit(solution)/shard_map/ppermute | solution.py:182
  67.8 14.5 %collective-permute-start.20 = (bf16[2,512,256]{2,1,0:T(8,128)(2,1)S(1)}, bf16[2,512,256]{2,1,0:T(8,128)(2,1)S(1)}, u32[]{:S(2)}, u32[]{:S(2)}) collective-permute-start(bf16[2,512,256]{2,1,0:T(8,128)(2,1)S(1)} %project.7), channel_id=1, source_target_pairs={{0,8},{1,17},{2,10},{3,19},{4,12},{5,21},{6,14},{7,23},{8,0},{9,25... | collective-permute-start | bytes 1572872 | tf_op jit(solution)/shard_map/ppermute | solution.py:182
  78.8 9.4 %collective-permute-start.13 = (bf16[512,256]{1,0:T(8,128)(2,1)S(1)}, bf16[512,256]{1,0:T(8,128)(2,1)S(1)}, u32[]{:S(2)}, u32[]{:S(2)}) collective-permute-start(bf16[512,256]{1,0:T(8,128)(2,1)S(1)} %fusion.2), channel_id=1, source_target_pairs={{0,8},{1,17},{2,10},{3,19},{4,12},{5,21},{6,14},{7,23},{8,0},{9,25... | collective-permute-start | bytes 786440 | tf_op jit(solution)/shard_map/ppermute | solution.py:182
  82.4 6.4 %collective-permute-start.21 = (bf16[512,256]{1,0:T(8,128)(2,1)S(1)}, bf16[512,256]{1,0:T(8,128)(2,1)S(1)}, u32[]{:S(2)}, u32[]{:S(2)}) collective-permute-start(bf16[512,256]{1,0:T(8,128)(2,1)S(1)} %fusion.3), channel_id=1, source_target_pairs={{0,16},{1,9},{2,18},{3,11},{4,20},{5,13},{6,22},{7,15},{8,24},{9,1... | collective-permute-start | bytes 786440 | tf_op jit(solution)/shard_map/ppermute | solution.py:182
  (2 other events, 4.5 us)
